TPU v7x, 32 devices: a whole 2x2x4 slice. The times are simulated.
32 devices in a mesh: tx: 8 (over y, x, core), ty: 4 (over z).
Axes of the slice: x: 2, y: 2, z: 4, core: 2. Of those that a mesh axis runs over, the one named last changes fastest.
Arguments:
- offsets: float32 [2, 16, 16, 128], P(None, 'tx', 'ty'), may hold values from 0 to 1
- circ: float32 [16, 16, 128], P('tx', 'ty'), as said below
- counts: int32 [16, 16], P('tx', 'ty'), may hold values from 1 to 128, as said below
Outputs:
- velocity: float32 [2, 16, 16, 128], P(None, 'tx', 'ty')
- moved: float32 [2, 16, 16, 128], P(None, 'tx', 'ty')
Inputs may be any that keep to these rules, and one draw needn't show every extreme that they name: counts of live slots in each cell; at least one cell holds 128; the middle quarter of the cell rows holds more on average. `circ`: circulations of order 0.02 / sqrt(128), of both signs.
All inputs are finite; a program needn't handle non-finite values.
Results may differ from a plain program's by a relative error of at most 0.00011.
Values sent between devices are 32-bit elements; how exact they have to be, the bound alone decides.
No kernel may reach another device: no remote copies, remote signals or barrier semaphores. Data moves between devices by JAX's collectives and lax.ppermute only.
A program may use at most 64 MiB of HBM per device.

v0:
```python
import math

import jax
import jax.numpy as jnp
from jax import lax
from jax.sharding import PartitionSpec as P

MODES = 64


two_pi = 2.0 * math.pi
screen = 1.5625
smooth = 0.0625
section_step = 0.25
all_shifts = ((-1, -1), (-1, 0), (-1, 1), (0, -1), (0, 0), (0, 1), (1, -1), (1, 0), (1, 1))


def extended(cells, sides, width):
    for axis, dim in sides:
        count = lax.axis_size(axis)
        head = lax.slice_in_dim(cells, 0, width, axis=dim)
        tail = lax.slice_in_dim(cells, cells.shape[dim] - width, cells.shape[dim], axis=dim)
        cells = jnp.concatenate(
            [
                lax.ppermute(tail, axis, [(i, (i + 1) % count) for i in range(count)]),
                cells,
                lax.ppermute(head, axis, [((i + 1) % count, i) for i in range(count)]),
            ],
            axis=dim,
        )
    return cells


def pair_sum(target, source, shift_rows, shift_cols):
    offset_x = target[0][:, :, None] - source[0][:, None, :] - shift_cols
    offset_y = target[1][:, :, None] - source[1][:, None, :] - shift_rows
    square = offset_x * offset_x + offset_y * offset_y
    weight = source[2][:, None, :] * jnp.exp(-screen * square) / (square + smooth)
    return jnp.stack([jnp.sum(-offset_y * weight, axis=2), jnp.sum(offset_x * weight, axis=2)])


def near_row(window, shift_list):
    span_cols = window.shape[2] - 2
    target = window[:, 1, 1 : 1 + span_cols]
    summed = jnp.zeros((2,) + target.shape[1:], jnp.float32)
    for shift_rows, shift_cols in shift_list:
        source = window[:, 1 + shift_rows, 1 + shift_cols : 1 + shift_cols + span_cols]
        summed = summed + pair_sum(target, source, float(shift_rows), float(shift_cols))
    return summed


def wave_numbers():
    return (jnp.arange(MODES, dtype=jnp.int32) - MODES // 2).astype(jnp.float32)


def mode_grid(cell_count):
    wave_number = wave_numbers()
    wave_x = two_pi * wave_number[:, None] * jnp.ones((1, MODES), jnp.float32)
    wave_y = two_pi * wave_number[None, :] * jnp.ones((MODES, 1), jnp.float32)
    square = wave_x * wave_x + wave_y * wave_y
    edge_mode = wave_number == -(MODES // 2)
    zero_mode = wave_number == 0
    keep_mode = jnp.logical_not(
        edge_mode[:, None] | edge_mode[None, :] | zero_mode[:, None] & zero_mode[None, :]
    )
    safe_square = jnp.where(keep_mode, square, 1.0)
    damping = jnp.where(
        keep_mode, jnp.exp(-safe_square / (6.25 * cell_count * cell_count)) / safe_square, 0.0
    )
    return (damping, wave_x, wave_y)


def tables(coord):
    phase_angle = two_pi * wave_numbers()[:, None] * coord[None, :]
    return (jnp.cos(phase_angle), jnp.sin(phase_angle))


def contract(left_side, right_side):
    return lax.dot_general(
        left_side,
        right_side,
        (((1,), (1,)), ((), ())),
        precision=lax.Precision.HIGHEST,
        preferred_element_type=jnp.float32,
    )


def product(left_side, right_side):
    return jnp.dot(
        left_side, right_side, precision=lax.Precision.HIGHEST, preferred_element_type=jnp.float32
    )


def structure(x_position, y_position, strength):
    cos_x, sin_x = tables(x_position)
    cos_y, sin_y = tables(y_position)
    real_part = contract(strength * cos_x, cos_y) - contract(strength * sin_x, sin_y)
    imag_part = contract(strength * sin_x, cos_y) + contract(strength * cos_x, sin_y)
    return jnp.stack([real_part, imag_part])


def mode_total(x_position, y_position, strength):
    partial_modes = structure(x_position, y_position, strength.reshape(-1))
    return lax.psum(partial_modes, ("tx", "ty"))


def far_velocity(x_position, y_position, scaled, wave_x, wave_y):
    cos_x, sin_x = tables(x_position)
    cos_y, sin_y = tables(y_position)
    with_imag = jnp.concatenate([wave_y * scaled[1], -wave_x * scaled[1]])
    with_real = jnp.concatenate([wave_y * scaled[0], -wave_x * scaled[0]])
    term_cos = (product(with_imag, cos_y) - product(with_real, sin_y)).reshape(2, MODES, -1)
    term_sin = (product(with_real, cos_y) + product(with_imag, sin_y)).reshape(2, MODES, -1)
    return jnp.sum(cos_x[None] * term_cos - sin_x[None] * term_sin, axis=1)


def ghost_cycle(packed):
    return extended(packed, (("tx", 1), ("ty", 2)), 1)


def per_device(offsets, circ, counts):
    rows_dev, cols_dev, slot_count = circ.shape
    cell_count = rows_dev * lax.axis_size("tx")
    live_slot = jnp.arange(slot_count, dtype=jnp.int32)[None, None, :] < counts[:, :, None]
    strength = jnp.where(live_slot, circ, 0.0)
    packed = jnp.stack([offsets[0], offsets[1], strength])
    row_start = lax.axis_index("tx") * rows_dev
    col_start = lax.axis_index("ty") * cols_dev
    row_pos = (row_start + jnp.arange(rows_dev, dtype=jnp.int32)).astype(jnp.float32)
    col_pos = (col_start + jnp.arange(cols_dev, dtype=jnp.int32)).astype(jnp.float32)
    x_position = ((col_pos[None, :, None] + offsets[0]) / cell_count).reshape(-1)
    y_position = ((row_pos[:, None, None] + offsets[1]) / cell_count).reshape(-1)
    damping, wave_x, wave_y = mode_grid(cell_count)
    row_list = jnp.arange(rows_dev, dtype=jnp.int32)
    padded = ghost_cycle(packed)
    near_part = lax.map(
        lambda first_row: near_row(lax.dynamic_slice_in_dim(padded, first_row, 3, 1), all_shifts),
        row_list,
    )
    summed = mode_total(x_position, y_position, strength)
    scaled = damping[None] * summed
    near_part = jnp.transpose(near_part, (1, 0, 2, 3)) * (cell_count / two_pi)
    far_part = far_velocity(x_position, y_position, scaled, wave_x, wave_y).reshape(
        2, rows_dev, cols_dev, slot_count
    )
    velocity = jnp.where(live_slot[None], near_part + far_part, 0.0)
    moved = offsets + section_step * velocity
    return (velocity, moved)


def solution(mesh):
    placed = (P(None, "tx", "ty", None), P("tx", "ty", None), P("tx", "ty"))
    return jax.shard_map(
        per_device,
        mesh=mesh,
        in_specs=placed,
        out_specs=(P(None, "tx", "ty", None), P(None, "tx", "ty", None)),
        check_vma=False,
    )
```

profile of v0, /device:TPU:0, one launch (start us, length us, event | category | flops | bytes accessed | tf_op | source)
XLA Modules:
  0.0 76.8 jit_solution(12997402943178533717)
XLA Ops:
  0.6 0.8 %fusion.101 = f32[1,2,4,128]{3,2,1,0:T(4,128)S(1)} fusion(f32[2,4,128]{2,1,0:T(4,128)} %param.6, s32[2,4]{1,0:T(2,128)} %param.7), kind=kLoop, calls=%fused_computation.209 | loop fusion | flops 2048 | bytes 8224 | tf_op jit(solution)/shard_map/stack | solution.py:126
  1.4 0.5 collective-permute-start
  2.0 2.9 %collective-permute-start.1 = (f32[3,1,4,128]{3,2,1,0:T(4,128)S(1)}, f32[3,1,4,128]{3,2,1,0:T(4,128)S(1)}, u32[]{:S(2)}, u32[]{:S(2)}) collective-permute-start(f32[3,1,4,128]{3,2,1,0:T(4,128)S(1)} %get-tuple-element.162), channel_id=1, source_target_pairs={{4,0},{8,4},{12,8},{16,12},{20,16},{24,20},{28,24},{0,28},{5,1},{9... | collective-permute-start | bytes 18440 | tf_op jit(solution)/shard_map/ppermute | solution.py:27
  4.9 0.7 copy-done.1
  5.8 2.1 %fusion.57 = f32[64,64]{1,0:T(8,128)S(1)} fusion(f32[1024]{0:T(1024)S(1)} %get-tuple-element.167, f32[1024]{0:T(1024)S(1)} %bitcast.171, f32[1024]{0:T(1024)S(1)} %get-tuple-element.168, f32[64]{0:T(128)S(1)} %convert_multiply_fusion), kind=kOutput, calls=%fused_computation.137 | convolution fusion | flops 50528256 | bytes 28928 | tf_op jit(solution)/shard_map/dot_general | solution.py:79
  8.0 2.1 %fusion.58 = f32[64,64]{1,0:T(8,128)S(1)} fusion(f32[1024]{0:T(1024)S(1)} %get-tuple-element.167, f32[1024]{0:T(1024)S(1)} %bitcast.172, f32[1024]{0:T(1024)S(1)} %get-tuple-element.168, f32[64]{0:T(128)S(1)} %convert_multiply_fusion), kind=kOutput, calls=%fused_computation.138 | convolution fusion | flops 50528256 | bytes 28928 | tf_op jit(solution)/shard_map/dot_general | solution.py:79
  10.1 2.1 %fusion.53 = f32[1,64,64]{2,1,0:T(8,128)S(1)} fusion(f32[64,64]{1,0:T(8,128)S(1)} %fusion.57, f32[1024]{0:T(1024)S(1)} %get-tuple-element.167, f32[1024]{0:T(1024)S(1)} %bitcast.173, f32[1024]{0:T(1024)S(1)} %get-tuple-element.168, f32[64]{0:T(128)S(1)} %convert_multiply_fusion), kind=kOutput, calls=%fused_computation.129 | convolution fusion | flops 50532352 | bytes 45312 | tf_op jit(solution)/shard_map/dot_general | solution.py:79
  12.3 2.1 %fusion.54 = f32[1,64,64]{2,1,0:T(8,128)S(1)} fusion(f32[64,64]{1,0:T(8,128)S(1)} %fusion.58, f32[1024]{0:T(1024)S(1)} %get-tuple-element.167, f32[1024]{0:T(1024)S(1)} %bitcast.174, f32[1024]{0:T(1024)S(1)} %get-tuple-element.168, f32[64]{0:T(128)S(1)} %convert_multiply_fusion), kind=kOutput, calls=%fused_computation.131 | convolution fusion | flops 50532352 | bytes 45312 | tf_op jit(solution)/shard_map/dot_general | solution.py:79
  14.4 40.8 %psum.7 = f32[2,64,64]{2,1,0:T(8,128)S(1)} all-reduce(f32[2,64,64]{2,1,0:T(8,128)S(1)} %pad_maximum_fusion), channel_id=1, replica_groups=mesh['tx'=8,'ty'=4] {'tx','ty'}, use_global_device_ids=true, to_apply=%region_20.21 | all-reduce | flops 8192 | bytes 65536 | tf_op jit(solution)/shard_map/psum | solution.py:104
  55.4 1.5 %fusion.56 = f32[128,1024]{1,0:T(8,128)S(1)} fusion(f32[1024]{0:T(1024)S(1)} %get-tuple-element.167, f32[64]{0:T(128)S(1)} %convert_multiply_fusion, f32[64,64]{1,0:T(8,128)S(1)} %get-tuple-element.158, f32[64,64]{1,0:T(8,128)S(1)} %get-tuple-element.153), kind=kOutput, calls=%fused_computation.136 | convolution fusion | flops 100737024 | bytes 561408 | tf_op jit(solution)/shard_map/dot_general | solution.py:89
  56.9 1.5 %fusion.55 = f32[128,1024]{1,0:T(8,128)S(1)} fusion(f32[1024]{0:T(1024)S(1)} %get-tuple-element.167, f32[64]{0:T(128)S(1)} %convert_multiply_fusion, f32[64,64]{1,0:T(8,128)S(1)} %get-tuple-element.157, f32[64,64]{1,0:T(8,128)S(1)} %get-tuple-element.154), kind=kOutput, calls=%fused_computation.135 | convolution fusion | flops 100737024 | bytes 561408 | tf_op jit(solution)/shard_map/dot_general | solution.py:89
  58.4 1.5 %convolution_subtract_fusion = f32[128,1024]{1,0:T(8,128)S(1)} fusion(f32[128,1024]{1,0:T(8,128)S(1)} %fusion.56, f32[1024]{0:T(1024)S(1)} %get-tuple-element.167, f32[64]{0:T(128)S(1)} %convert_multiply_fusion, f32[64,64]{1,0:T(8,128)S(1)} %get-tuple-element.157, f32[64,64]{1,0:T(8,128)S(1)} %get-tuple-element.154), kind=kOutput, calls=%fused_computation.127 | convolution fusion | flops 100868096 | bytes 1085696 | tf_op jit(solution)/shard_map/dot_general | solution.py:89
  59.9 1.0 %multiply_cosine_fusion.5 = (f32[64,1024]{1,0:T(8,128)S(1)}, f32[64,1024]{1,0:T(8,128)S(1)}) fusion(f32[1024]{0:T(1024)S(1)} %get-tuple-element.168, f32[64]{0:T(128)S(1)} %convert_multiply_fusion), kind=kLoop, calls=%fused_computation.140 | loop fusion | flops 65536 | bytes 528640 | tf_op jit(solution)/shard_map/cos | solution.py:75
  60.9 1.6 %collective-permute-start.2 = (f32[3,4,1,128]{3,2,1,0:T(1,128)S(1)}, f32[3,4,1,128]{3,2,1,0:T(1,128)S(1)}, u32[]{:S(2)}, u32[]{:S(2)}) collective-permute-start(f32[3,4,1,128]{3,2,1,0:T(1,128)S(1)} %get-tuple-element.159), channel_id=1, source_target_pairs={{0,1},{1,2},{2,3},{3,0},{4,5},{5,6},{6,7},{7,4},{8,9},{9,10},{10,1... | collective-permute-start | bytes 18440 | tf_op jit(solution)/shard_map/ppermute | solution.py:25
  62.5 2.3 %collective-permute-start.3 = (f32[3,4,1,128]{3,2,1,0:T(1,128)S(1)}, f32[3,4,1,128]{3,2,1,0:T(1,128)S(1)}, u32[]{:S(2)}, u32[]{:S(2)}) collective-permute-start(f32[3,4,1,128]{3,2,1,0:T(1,128)S(1)} %get-tuple-element.160), channel_id=1, source_target_pairs={{1,0},{2,1},{3,2},{0,3},{5,4},{6,5},{7,6},{4,7},{9,8},{10,9},{11,1... | collective-permute-start | bytes 18440 | tf_op jit(solution)/shard_map/ppermute | solution.py:27
  64.9 1.5 %subtract_reduce_fusion = f32[2,1024]{1,0:T(2,128)S(1)} fusion(f32[64,1024]{1,0:T(8,128)S(1)} %get-tuple-element.166, f32[64,1024]{1,0:T(8,128)S(1)} %get-tuple-element.165, f32[128,1024]{1,0:T(8,128)S(1)} %convolution_subtract_fusion, f32[128,1024]{1,0:T(8,128)S(1)} %fusion.55, f32[1024]{0:T(1024)S(1)} %get-tuple-element.167, ...), kind=kOutput, calls=%fused_computation.132 | convolution fusion | flops 101390336 | bytes 1618176 | tf_op jit(solution)/shard_map/dot_general | solution.py:89
  66.5 9.7 %while.13 = (s32[]{:T(128)}, f32[2,2,4,128]{3,2,0,1:T(4,128)S(1)}, s32[2]{0:T(128)S(1)}, f32[3,4,6,128]{3,2,1,0:T(8,128)S(1)}, s32[]{:T(128)}, /*index=5*/s32[]{:T(128)}, s32[]{}, s32[]{:T(128)}, s32[]{}) while((s32[]{:T(128)}, f32[2,2,4,128]{3,2,0,1:T(4,128)S(1)}, s32[2]{0:T(128)S(1)}, f32[3,4,6,128]{3,2,1,0:T(8,128)S(1)}, s32[]{:T(128)}, ...), condition=%wide.region_19.20_spmd, body=%wide.region_0.19_spmd.sunk | while | flops 9052169 | bytes 248019 | solution.py:136
  66.5 0.6 dynamic_slice.16
  69.1 1.2 %multiply_reduce_fusion.15 = (f32[4,128]{1,0:T(4,128)S(1)}, f32[4,128]{1,0:T(4,128)S(1)}, f32[4,128]{1,0:T(4,128)S(1)}, f32[4,128]{1,0:T(4,128)S(1)}, f32[4,128]...) fusion(f32[4,128]{1,0:T(4,128)S(1)} %get-tuple-element.258, ...), kind=kLoop, calls=%fused_computation.59.clone.1 | loop fusion | flops 5957632 | bytes 61440 | tf_op jit(solution)/shard_map/while/body/eval_jaxpr/reduce_sum | solution.py:39
  70.3 0.9 %multiply_reduce_fusion.14 = (f32[4,128]{1,0:T(4,128)S(1)}, f32[4,128]{1,0:T(4,128)S(1)}, f32[4,128]{1,0:T(4,128)S(1)}, f32[4,128]{1,0:T(4,128)S(1)}, f32[4,128]{1,0:T(4,128)S(1)}, /*index=5*/f32[4,128]{1,0:T(4,128)S(1)}) fusion(f32[4,128]{1,0:T(4,128)S(1)} %get-tuple-element.241, f32[4,128]{1,0:T(4,128)S(1)} %get-tuple-element.242, ...), kind=kLoop, calls=%fused_computation.40.clone.1 | loop fusion | flops 3077120 | bytes 34816 | tf_op jit(solution)/shard_map/while/body/eval_jaxpr/reduce_sum | solution.py:39
  71.3 0.6 dynamic_slice.16
  73.9 1.2 %multiply_reduce_fusion.15 = (f32[4,128]{1,0:T(4,128)S(1)}, f32[4,128]{1,0:T(4,128)S(1)}, f32[4,128]{1,0:T(4,128)S(1)}, f32[4,128]{1,0:T(4,128)S(1)}, f32[4,128]...) fusion(f32[4,128]{1,0:T(4,128)S(1)} %get-tuple-element.258, ...), kind=kLoop, calls=%fused_computation.59.clone.1 | loop fusion | flops 5957632 | bytes 61440 | tf_op jit(solution)/shard_map/while/body/eval_jaxpr/reduce_sum | solution.py:39
  75.2 0.9 %multiply_reduce_fusion.14 = (f32[4,128]{1,0:T(4,128)S(1)}, f32[4,128]{1,0:T(4,128)S(1)}, f32[4,128]{1,0:T(4,128)S(1)}, f32[4,128]{1,0:T(4,128)S(1)}, f32[4,128]{1,0:T(4,128)S(1)}, /*index=5*/f32[4,128]{1,0:T(4,128)S(1)}) fusion(f32[4,128]{1,0:T(4,128)S(1)} %get-tuple-element.241, f32[4,128]{1,0:T(4,128)S(1)} %get-tuple-element.242, ...), kind=kLoop, calls=%fused_computation.40.clone.1 | loop fusion | flops 3077120 | bytes 34816 | tf_op jit(solution)/shard_map/while/body/eval_jaxpr/reduce_sum | solution.py:39
  76.2 0.6 multiply_add_fusion
  (35 shorter events, 0.8 us)
Async XLA Ops:
  0.6 0.8 %copy-start = (f32[2,2,4,128]{3,2,1,0:T(4,128)S(1)}, f32[2,2,4,128]{3,2,1,0:T(4,128)}, u32[]{:S(2)}) copy-start(f32[2,2,4,128]{3,2,1,0:T(4,128)} %param.5) | copy-start | bytes 24580
  1.4 59.4 %collective-permute-start = (f32[3,1,4,128]{3,2,1,0:T(4,128)S(1)}, f32[3,1,4,128]{3,2,1,0:T(4,128)S(1)}, u32[]{:S(2)}, u32[]{:S(2)}) collective-permute-start(f32[3,1,4,128]{3,2,1,0:T(4,128)S(1)} %get-tuple-element.161), channel_id=1, source_target_pairs={{0,4},{4,8},{8,12},{12,16},{16,20},{20,24},{24,28},{28,0},{1,5},{5... | collective-permute-start | bytes 18440 | tf_op jit(solution)/shard_map/ppermute | solution.py:25
  2.0 58.9 %collective-permute-start.1 = (f32[3,1,4,128]{3,2,1,0:T(4,128)S(1)}, f32[3,1,4,128]{3,2,1,0:T(4,128)S(1)}, u32[]{:S(2)}, u32[]{:S(2)}) collective-permute-start(f32[3,1,4,128]{3,2,1,0:T(4,128)S(1)} %get-tuple-element.162), channel_id=1, source_target_pairs={{4,0},{8,4},{12,8},{16,12},{20,16},{24,20},{28,24},{0,28},{5,1},{9... | collective-permute-start | bytes 18440 | tf_op jit(solution)/shard_map/ppermute | solution.py:27
  4.9 0.7 copy-start.1
  4.9 0.7 copy-start.2
  60.9 5.5 %collective-permute-start.2 = (f32[3,4,1,128]{3,2,1,0:T(1,128)S(1)}, f32[3,4,1,128]{3,2,1,0:T(1,128)S(1)}, u32[]{:S(2)}, u32[]{:S(2)}) collective-permute-start(f32[3,4,1,128]{3,2,1,0:T(1,128)S(1)} %get-tuple-element.159), channel_id=1, source_target_pairs={{0,1},{1,2},{2,3},{3,0},{4,5},{5,6},{6,7},{7,4},{8,9},{9,10},{10,1... | collective-permute-start | bytes 18440 | tf_op jit(solution)/shard_map/ppermute | solution.py:25
  62.5 4.0 %collective-permute-start.3 = (f32[3,4,1,128]{3,2,1,0:T(1,128)S(1)}, f32[3,4,1,128]{3,2,1,0:T(1,128)S(1)}, u32[]{:S(2)}, u32[]{:S(2)}) collective-permute-start(f32[3,4,1,128]{3,2,1,0:T(1,128)S(1)} %get-tuple-element.160), channel_id=1, source_target_pairs={{1,0},{2,1},{3,2},{0,3},{5,4},{6,5},{7,6},{4,7},{9,8},{10,9},{11,1... | collective-permute-start | bytes 18440 | tf_op jit(solution)/shard_map/ppermute | solution.py:27
where the time goes:
time: 77.2 us; the launch traced here: 76.8 us
  blocking collectives  40.8 us (53%)
  matrix products  14.5 us (19%)
  starting transfers between devices  7.36 us (10%)
  other arithmetic  7.21 us (9%)
  loops' own time  3.95 us (5%)
  local copies, waits for them, and re-layouts  2.17 us (3%)
  between operations  0.83 us (1%)
    psum x1, blocking collectives, mode_total(): return lax.psum(partial_modes, ('tx', 'ty'))  40.8 us
    dot_general x4, matrix products, contract(): lax.dot_general(left_side, right_side, (((1,), (1,)), ((), ())), precisio...  8.51 us
    dot_general x4, matrix products, product(): jnp.dot(left_side, right_side, precision=lax.Precision.HIGHEST, preferred...  5.95 us
    ppermute x2, starting transfers between devices, extended(): lax.ppermute(head, axis, [((i + 1) % count, i) for i in range(count)])  5.26 us
    reduce_sum x4, other arithmetic, pair_sum(): jnp.sum(-offset_y * weight, axis=2)  4.36 us
    another operation x1, loops' own time, per_device(): lax.map(lambda first_row: near_row(lax.dynamic_slice_in_dim(padded, first...  3.95 us
    ppermute x2, starting transfers between devices, extended(): lax.ppermute(tail, axis, [(i, (i + 1) % count) for i in range(count)])  2.1 us
  transfers between devices with their start and end apart: 4, of which 0 were waited for; matrix products, arithmetic and copies ran while one was open for 21% of the time, Pallas kernels for 0%

commit v1 on v0

v1 whole, which is shorter than its diff:
```python
import functools
import math

import jax
import jax.numpy as jnp
from jax import lax
from jax.experimental import pallas as pl
from jax.experimental.pallas import tpu as pltpu
from jax.sharding import PartitionSpec as P


MODES = 64
HALF = MODES // 2

two_pi = 2.0 * math.pi
screen = 1.5625
smooth = 0.0625
section_step = 0.25
unit = math.sqrt(screen / math.log(2.0))
floor_term = smooth * unit * unit

VMEM = pl.BlockSpec(memory_space=pltpu.VMEM)
SMEM = pl.BlockSpec(memory_space=pltpu.SMEM)
PARAMS = pltpu.CompilerParams(vmem_limit_bytes=8 * 1024 * 1024)


def call(body, out_shapes, scratch, flops, *args):
    specs = [SMEM if a.dtype == jnp.int32 else VMEM for a in args]
    outs = [jax.ShapeDtypeStruct(s, d) for s, d in out_shapes]
    return pl.pallas_call(
        body,
        out_shape=outs,
        in_specs=specs,
        out_specs=[VMEM] * len(outs),
        scratch_shapes=scratch,
        compiler_params=PARAMS,
        cost_estimate=pl.CostEstimate(flops=flops, bytes_accessed=65536, transcendentals=0),
    )(*args)


def cell_rows(ref, rows):
    return jnp.concatenate([ref[r] for r in range(rows)], axis=0)


def count_grid(counts_ref, rows, cols, shape):
    cell = lax.broadcasted_iota(jnp.int32, shape, 0)
    limit = jnp.zeros(shape, jnp.int32)
    for r in range(rows):
        for c in range(cols):
            limit = jnp.where(cell == r * cols + c, counts_ref[r, c], limit)
    return lax.broadcasted_iota(jnp.int32, shape, 1) < limit


def unit_circle(turn):
    quarter = jnp.floor(4.0 * turn + 0.5)
    angle = two_pi * (turn - 0.25 * quarter)
    sq = angle * angle
    sine = angle * (
        1.0 + sq * (-1.0 / 6 + sq * (1.0 / 120 + sq * (-1.0 / 5040 + sq * (1.0 / 362880))))
    )
    cosine = 1.0 + sq * (
        -0.5 + sq * (1.0 / 24 + sq * (-1.0 / 720 + sq * (1.0 / 40320 + sq * (-1.0 / 3628800))))
    )
    odd = (quarter == 1.0) | (quarter == 3.0)
    cos_neg = (quarter == 1.0) | (quarter == 2.0)
    sin_neg = (quarter == 2.0) | (quarter == 3.0)
    cos_part = jnp.where(odd, sine, cosine)
    sin_part = jnp.where(odd, cosine, sine)
    return jnp.where(cos_neg, -cos_part, cos_part), jnp.where(sin_neg, -sin_part, sin_part)


def times(p, q):
    return p[0] * q[0] - p[1] * q[1], p[0] * q[1] + p[1] * q[0]


def split(value):
    high = value.astype(jnp.bfloat16)
    low = (value - high.astype(jnp.float32)).astype(jnp.bfloat16)
    return high, low


def moments_kernel(
    rows, cols, cell_count, place, offsets, counts, circ, own, x_table, y_table, powers, weighted
):
    cells = rows * cols
    slots = circ.shape[2]
    shape = (cells, slots)
    cell = lax.broadcasted_iota(jnp.int32, shape, 0)
    row_in = jnp.zeros(shape, jnp.int32)
    for r in range(1, rows):
        row_in = jnp.where(cell >= r * cols, r, row_in)
    col_in = cell - row_in * cols
    live = count_grid(counts, rows, cols, shape)
    strength = jnp.where(live, cell_rows(circ, rows), 0.0)
    off_x = cell_rows(offsets.at[0], rows)
    off_y = cell_rows(offsets.at[1], rows)
    x_turn = ((place[1] * cols + col_in).astype(jnp.float32) + off_x) / cell_count
    y_turn = ((place[0] * rows + row_in).astype(jnp.float32) + off_y) / cell_count
    own[4] = unit * (col_in.astype(jnp.float32) + off_x)
    own[5] = unit * ((place[2] * rows + row_in).astype(jnp.float32) + off_y)
    own[6] = strength * (unit * cell_count / two_pi)
    for axis, turn in ((0, x_turn), (1, y_turn)):
        point = unit_circle(turn)
        for power in range(5):
            powers[axis, power, 0] = point[0]
            powers[axis, power, 1] = point[1]
            if power < 4:
                point = times(point, point)
    powers[0, 0, 2] = strength
    mode = lax.broadcasted_iota(jnp.int32, (8, slots), 0)
    bits = [(mode & (1 << b)) != 0 for b in range(3)]
    for i in range(cells):
        lanes = pl.ds(i * slots, slots)
        amount = jnp.broadcast_to(powers[0, 0, 2, pl.ds(i, 1), :], (8, slots))
        for axis in range(2):

            def row(power, part):
                return jnp.broadcast_to(powers[axis, power, part, pl.ds(i, 1), :], (8, slots))

            group = None
            for b in range(3):
                factor = (jnp.where(bits[b], row(b, 0), 1.0), jnp.where(bits[b], row(b, 1), 0.0))
                group = factor if group is None else times(group, factor)
            eight = (row(3, 0), row(3, 1))
            sixteen = (row(4, 0), row(4, 1))
            second = times(group, eight)
            groups = [group, second, times(group, sixteen), times(second, sixteen)]
            wave = jnp.concatenate([g[0] for g in groups] + [g[1] for g in groups], axis=0)
            if axis == 0:
                x_table[:, lanes] = wave
                high, low = split(wave * jnp.concatenate([amount] * 8, axis=0))
                weighted[0:MODES, lanes] = high
                weighted[MODES : 2 * MODES, lanes] = low
            else:
                high, low = split(wave)
                y_table[0:MODES, lanes] = high
                y_table[MODES : 2 * MODES, lanes] = low
    full = lax.dot_general(
        weighted[...],
        y_table[...],
        (((1,), (1,)), ((), ())),
        preferred_element_type=jnp.float32,
    )
    full = full[0:MODES] + full[MODES : 2 * MODES]
    full = full + pltpu.roll(full, MODES, 1)
    lane = lax.broadcasted_iota(jnp.int32, (HALF, 2 * MODES), 1)
    own[0:4] = jnp.where(lane < MODES, full[0:HALF], full[HALF:MODES]).reshape(4, 8, 2 * MODES)


def pair_terms(target, source, total):
    offset_x = target[0] - source[0]
    offset_y = target[1] - source[1]
    square = offset_x * offset_x + offset_y * offset_y
    weight = source[2] / ((square + floor_term) * jnp.exp2(square))
    return total[0] - offset_y * weight, total[1] + offset_x * weight


def near_sum(sources, targets, links, turned):
    slots = sources[0][0].shape[1]
    stack = [part for source in sources for part in source]
    pad = -len(stack) % 8
    stack = jnp.concatenate(stack + [jnp.zeros((pad, slots), jnp.float32)] * (pad > 0), axis=0)
    turned[:, 0 : stack.shape[0]] = stack.T
    spread = [tuple(jnp.broadcast_to(part, (8, slots)) for part in t) for t in targets]

    def step(k, totals):
        totals = list(totals)
        chunk = turned[pl.ds(pl.multiple_of(8 * k, 8), 8), :]
        for i, reached in enumerate(links):
            source = tuple(
                jnp.broadcast_to(chunk[:, 3 * i + part : 3 * i + part + 1], (8, slots))
                for part in range(3)
            )
            for t in reached:
                totals[2 * t], totals[2 * t + 1] = pair_terms(
                    spread[t], source, (totals[2 * t], totals[2 * t + 1])
                )
        return tuple(totals)

    zero = jnp.zeros((8, slots), jnp.float32)
    totals = (zero,) * (2 * len(targets))
    totals = lax.fori_loop(
        0, slots // 16, lambda k, held: step(2 * k + 1, step(2 * k, held)), totals
    )
    return [jnp.sum(total, axis=0, keepdims=True) for total in totals]


def reach(col, cols):
    return [c for c in (col - 1, col, col + 1) if 0 <= c < cols]


def read_row(ref, base, at):
    return tuple(ref[base + part, pl.ds(at, 1), :] for part in range(3))


def near_local(rows, cols, own, cells, near, turned):
    places = sorted({(r, c) for row, col in cells for r in range(rows) if abs(r - row) <= 1 for c in reach(col, cols)})
    sources = [read_row(own, 4, r * cols + c) for r, c in cells]
    targets = [read_row(own, 4, r * cols + c)[:2] for r, c in places]
    links = [
        [t for t, (r, c) in enumerate(places) if abs(r - row) <= 1 and abs(c - col) <= 1]
        for row, col in cells
    ]
    sums = near_sum(sources, targets, links, turned)
    for t, (r, c) in enumerate(places):
        for part in range(2):
            at = pl.ds(r * cols + c, 1)
            near[part, at, :] = near[part, at, :] + sums[2 * t + part]


def near_local_kernel(rows, cols, cells, own, near, turned):
    near[...] = jnp.zeros_like(near)
    near_local(rows, cols, own, cells, near, turned)


def near_rows(rows, cols, own, outer, base, above, near, turned):
    def pick(ref, origin, part, first, second):
        return jnp.where(
            above == 1, ref[origin + part, pl.ds(first, 1), :], ref[origin + part, pl.ds(second, 1), :]
        )

    sources = [
        tuple(pick(outer, base, part, cols + c, c) for part in range(3)) for c in range(cols)
    ]
    last = (rows - 1) * cols
    targets = [tuple(pick(own, 4, part, c, last + c) for part in range(2)) for c in range(cols)]
    sums = near_sum(sources, targets, [reach(c, cols) for c in range(cols)], turned)
    top = jnp.where(above == 1, 0, last)
    for c in range(cols):
        for part in range(2):
            at = pl.ds(top + c, 1)
            near[part, at, :] = near[part, at, :] + sums[2 * c + part]


def near_cols(rows, cols, own, side, base, core, right, near, turned):
    shift = jnp.where(right == 1, unit * cols, -unit * cols)
    sources = []
    for k in range(rows + 2):
        row = read_row(side, base, core * rows + k)
        sources.append((row[0] + shift, row[1], row[2]))
    edge = jnp.where(right == 1, cols - 1, 0)
    targets = [read_row(own, 4, r * cols + edge)[:2] for r in range(rows)]
    links = [[r for r in range(rows) if 0 <= k - r <= 2] for k in range(rows + 2)]
    sums = near_sum(sources, targets, links, turned)
    for r in range(rows):
        for part in range(2):
            at = pl.ds(r * cols + edge, 1)
            near[part, at, :] = near[part, at, :] + sums[2 * r + part]


def near_partner_kernel(rows, cols, cells, place, own, partner, near, turned):
    near[...] = jnp.zeros_like(near)
    near_local(rows, cols, own, cells, near, turned)
    near_rows(rows, cols, own, partner, 4, place[2], near, turned)


def near_ring_kernel(rows, cols, place, own, packed, near, turned):
    near[...] = jnp.zeros_like(near)
    near_rows(rows, cols, own, packed, 10, 1 - place[2], near, turned)


def near_close_kernel(rows, cols, place, own, close, near, turned):
    near[...] = jnp.zeros_like(near)
    right = 1 - lax.rem(place[1], 2)
    near_cols(rows, cols, own, close, 0, place[2], right, near, turned)


def pack_kernel(rows, cols, place, own, partner, ring, packed):
    core = place[2]
    packed[4:10] = jnp.zeros((6,) + packed.shape[1:], jnp.float32)
    packed[0:4] = ring[0:4]
    for edge, col in ((0, 0), (1, cols - 1)):
        for part in range(3):
            at = 4 + 3 * edge + part
            packed[at, pl.ds(0, 1), :] = ring[4 + part, pl.ds(cols + col, 1), :]
            for r in range(rows):
                cell = pl.ds(r * cols + col, 1)
                packed[at, pl.ds(1 + rows * core + r, 1), :] = own[4 + part, cell, :]
                packed[at, pl.ds(1 + rows * (1 - core) + r, 1), :] = partner[4 + part, cell, :]
            packed[at, pl.ds(1 + 2 * rows, 1), :] = ring[4 + part, pl.ds(col, 1), :]
    packed[10:13] = ring[4:7]


def final_kernel(
    rows, cols, cell_count, place, offsets, counts, own, x_table, y_table, last,
    near_a, near_b, near_c, near_d, near_e, velocity, moved, near, far, turned,
):
    cells = rows * cols
    slots = own.shape[2]
    core = place[2]
    shape = (HALF, 2 * MODES)
    lane = lax.broadcasted_iota(jnp.int32, shape, 1)
    m = lax.broadcasted_iota(jnp.int32, shape, 0).astype(jnp.float32)
    n = (lane & (HALF - 1)).astype(jnp.float32)
    square = (two_pi * two_pi) * (m * m + n * n)
    keep = square > 0.0
    safe = jnp.where(keep, square, 1.0)
    damping = jnp.where(keep, jnp.exp(-safe / (6.25 * cell_count * cell_count)) / safe, 0.0)
    damping = damping * (4.0 * two_pi)
    u_weight = damping * n * jnp.where(m == 0.0, 0.5, 1.0)
    v_weight = damping * m * jnp.where(n == 0.0, 0.5, 1.0)
    total = last[0:4].reshape(shape)
    y_odd = (lane & HALF) != 0
    swapped = jnp.where(y_odd, -pltpu.roll(total, HALF, 1), pltpu.roll(total, 2 * MODES - HALF, 1))
    u_part = u_weight * swapped
    crossed = pltpu.roll(total, MODES, 1)
    v_part = v_weight * jnp.where(lane < MODES, -crossed, crossed)
    left = []
    for part in (u_part, v_part):
        other = pltpu.roll(part, MODES, 1)
        for doubled in (
            jnp.where(lane < MODES, part, other),
            jnp.where(lane < MODES, other, part),
        ):
            left.append(jnp.concatenate(split(doubled), axis=1))
    left = jnp.concatenate(left, axis=0)
    right = jnp.concatenate([y_table[...], y_table[...]], axis=0)
    terms = jnp.dot(left, right, preferred_element_type=jnp.float32)
    for i in range(cells):
        lanes = slice(i * slots, (i + 1) * slots)
        wave = x_table[:, lanes]
        far[0, pl.ds(i, 1), :] = jnp.sum(terms[0:MODES, lanes] * wave, axis=0, keepdims=True)
        far[1, pl.ds(i, 1), :] = jnp.sum(terms[MODES:, lanes] * wave, axis=0, keepdims=True)
    near[...] = (near_a[...] + near_b[...]) + (near_c[...] + near_d[...]) + near_e[...]
    near_cols(rows, cols, own, last, 4, core, lax.rem(place[1], 2), near, turned)
    live = count_grid(counts, rows, cols, (cells, slots))
    for part in range(2):
        value = jnp.where(live, near[part] + far[part], 0.0)
        for r in range(rows):
            piece = value[r * cols : (r + 1) * cols]
            velocity[part, r] = piece
            moved[part, r] = offsets[part, r] + section_step * piece


def far_item(items, index):
    count = 1 << (len(items) - 1)
    up = jnp.where(index % 2 == 1, (index + 1) % count, (index + count - 1) % count)
    mask = index ^ up
    chosen = items[-1]
    for k in range(2, len(items) - 1):
        chosen = jnp.where(mask == (1 << k) - 1, items[k], chosen)
    return chosen


def per_device(offsets, circ, counts):
    rows, cols, slots = circ.shape
    cells = rows * cols
    tx_size, ty_size = lax.axis_size("tx"), lax.axis_size("ty")
    chips = tx_size // 2
    cell_count = rows * tx_size
    tx, ty = lax.axis_index("tx"), lax.axis_index("ty")
    core, chip = tx % 2, tx // 2
    place = jnp.stack([tx, ty, core]).astype(jnp.int32)
    f32, bf16 = jnp.float32, jnp.bfloat16
    turned = [pltpu.VMEM((slots, 128), f32)]
    near_shape = [((2, cells, slots), f32)]

    own, x_table, y_table = call(
        functools.partial(moments_kernel, rows, cols, cell_count),
        [((7, cells, slots), f32), ((MODES, cells * slots), f32), ((2 * MODES, cells * slots), bf16)],
        [pltpu.VMEM((2, 5, 3, cells, slots), f32), pltpu.VMEM((2 * MODES, cells * slots), bf16)],
        4_000_000,
        place, offsets, counts, circ,
    )

    def swap(message, chip_bit, column_bit):
        pairs = [
            (i * ty_size + q, ((i // 2 ^ chip_bit) * 2 + (i + 1) % 2) * ty_size + (q ^ column_bit))
            for i in range(tx_size)
            for q in range(ty_size)
        ]
        return lax.ppermute(message, ("tx", "ty"), pairs)

    def near_call(body, flops, *args):
        return call(body, near_shape, turned, flops, *args)[0]

    whole = [(r, c) for c in range(cols) for r in range(rows)]
    third = len(whole) // 4
    partner = swap(own, 0, 0)
    near_a = near_call(
        functools.partial(near_local_kernel, rows, cols, whole[:third]), 4_000_000, own
    )
    total = own[0:4] + partner[0:4]
    first = jnp.where(core == 0, own[4:7], partner[4:7])
    second = jnp.where(core == 0, partner[4:7], own[4:7])
    items = [jnp.concatenate([first[:, 0:cols], second[:, cells - cols : cells]], axis=1)]
    bit = 1
    while bit < chips:
        message = jnp.concatenate([total, items[-1]], axis=0)
        got = swap(message, bit, 0)
        total = total + got[0:4]
        items.append(got[4:7])
        bit *= 2
    near_b = near_call(
        functools.partial(near_local_kernel, rows, cols, whole[third : 3 * third]), 9_000_000, own
    )
    near_c = near_call(
        functools.partial(near_partner_kernel, rows, cols, whole[3 * third :]), 9_000_000,
        place, own, partner,
    )
    slot_of = lax.broadcasted_iota(jnp.int32, (3, 2 * cols, slots), 1)
    below = slot_of < cols
    distant = far_item(items, chip) if chips > 2 else items[1]
    ring = jnp.where(below == (chip % 2 == 0), items[1], distant)
    shift = jnp.where(below, 2.0 * rows * unit, -2.0 * rows * unit)
    which = lax.broadcasted_iota(jnp.int32, (3, 2 * cols, slots), 0)
    ring = ring + jnp.where(which == 1, shift, 0.0)
    (packed,) = call(
        functools.partial(pack_kernel, rows, cols), [((13, cells, slots), f32)], [], 100_000,
        place, own, partner, jnp.concatenate([total, ring], axis=0),
    )
    got = swap(packed, 0, 1)
    near_d = near_call(
        functools.partial(near_ring_kernel, rows, cols), 5_000_000, place, own, packed
    )
    total = packed[0:4] + got[0:4]
    close = jnp.where(ty % 2 == 0, got[4:7], got[7:10])
    items = [None, jnp.where(ty % 2 == 0, got[7:10], got[4:7])]
    bit = 2
    while bit < ty_size:
        message = jnp.concatenate([total, items[-1]], axis=0)
        got = swap(message, 0, bit)
        total = total + got[0:4]
        items.append(got[4:7])
        bit *= 2
    near_e = near_call(
        functools.partial(near_close_kernel, rows, cols), 3_000_000, place, own, close
    )
    distant = far_item(items, ty) if ty_size > 2 else items[1]
    last = jnp.concatenate([total, distant], axis=0)
    return tuple(
        call(
            functools.partial(final_kernel, rows, cols, cell_count),
            [(offsets.shape, f32)] * 2,
            [pltpu.VMEM((2, cells, slots), f32), pltpu.VMEM((2, cells, slots), f32)] + turned,
            4_000_000,
            place, offsets, counts, own, x_table, y_table, last,
            near_a, near_b, near_c, near_d, near_e,
        )
    )


def solution(mesh):
    placed = (P(None, "tx", "ty", None), P("tx", "ty", None), P("tx", "ty"))

    return jax.shard_map(
        per_device,
        mesh=mesh,
        in_specs=placed,
        out_specs=(P(None, "tx", "ty", None), P(None, "tx", "ty", None)),
        check_vma=False,
    )
```

time: 77.2 us -> 29.7 us (0.38)
  blocking collectives: 40.8 us -> 0 us
  matrix products: 14.5 us -> 0 us
  Pallas kernels: 0 us -> 12.1 us
  other arithmetic: 7.21 us -> 0.23 us
  waiting for transfers between devices: 0.01 us -> 5.84 us
  loops' own time: 3.95 us -> 0 us
  starting transfers between devices: 7.36 us -> 9.89 us
  local copies, waits for them, and re-layouts: 2.17 us -> 0.61 us
    psum x1 -> x0, blocking collectives: 40.8 us -> none  [mode_total(): return lax.psum(partial_modes, ('tx', 'ty'))]
    dot_general x8 -> x0, matrix products: 14.5 us -> none  [the longest x4 8.51 us: contract(): lax.dot_general(left_side, right_side, (((1,), (1,)), ((), ())), precisio...]
    pallas_call x0 -> x8, Pallas kernels: none -> 12.1 us  [call(): pl.pallas_call(body, out_shape=outs, in_specs=specs, out_specs=[VMEM] * l...]
    ppermute x4 -> x5, waiting for transfers between devices: 0.01 us -> 5.84 us  [swap(): return lax.ppermute(message, ('tx', 'ty'), pairs)]
    reduce_sum x4 -> x0, other arithmetic: 4.36 us -> none  [pair_sum(): jnp.sum(-offset_y * weight, axis=2)]
    another operation x1 -> x0, loops' own time: 3.95 us -> none  [per_device(): lax.map(lambda first_row: near_row(lax.dynamic_slice_in_dim(padded, first...]
    ppermute x4 -> x5, starting transfers between devices: 7.36 us -> 9.89 us  [swap(): return lax.ppermute(message, ('tx', 'ty'), pairs)]
    dynamic_slice x2 -> x0, local copies, waits for them, and re-layouts: 1.18 us -> none  [per_device(): lax.map(lambda first_row: near_row(lax.dynamic_slice_in_dim(padded, first...]
  transfers between devices with their start and end apart: 4 -> 5, of which waited for: 0 -> 4; matrix products, arithmetic and copies ran while one was open for 21% -> 0% of each run, Pallas kernels for 0% -> 27%
where the time goes in v1:
time: 29.7 us; the launch traced here: 29.5 us
  Pallas kernels  12.1 us (41%)
  starting transfers between devices  9.89 us (33%)
  waiting for transfers between devices  5.84 us (20%)
  between operations  0.79 us (3%)
  local copies, waits for them, and re-layouts  0.61 us (2%)
    pallas_call x8, Pallas kernels, call(): pl.pallas_call(body, out_shape=outs, in_specs=specs, out_specs=[VMEM] * l...  12.1 us
    ppermute x5, starting transfers between devices, swap(): return lax.ppermute(message, ('tx', 'ty'), pairs)  9.89 us
    ppermute x5, waiting for transfers between devices, swap(): return lax.ppermute(message, ('tx', 'ty'), pairs)  5.84 us
    unnamed x6, local copies, waits for them, and re-layouts  0.6 us
  transfers between devices with their start and end apart: 5, of which 4 were waited for; matrix products, arithmetic and copies ran while one was open for 0% of the time, Pallas kernels for 27%

profile of v1, /device:TPU:0, one launch (start us, length us, event | category | flops | bytes accessed | tf_op | source)
XLA Modules:
  0.0 29.5 jit_solution(9991019902086142139)
XLA Ops:
  0.6 0.0 copy-start
  0.7 0.1 pad_add_fusion.place
  0.8 0.6 %copy-done = f32[2,2,4,128]{3,2,1,0:T(4,128)S(1)} copy-done((f32[2,2,4,128]{3,2,1,0:T(4,128)S(1)}, f32[2,2,4,128]{3,2,1,0:T(4,128)}, u32[]{:S(2)}) %copy-start) | copy-done | bytes 8216
  1.3 0.0 copy-done.2
  1.3 0.0 copy-done.1
  1.4 1.0 %shard_map.50 = (f32[7,8,128]{2,1,0:T(8,128)S(1)}, f32[64,1024]{1,0:T(8,128)S(1)}, bf16[128,1024]{1,0:T(8,128)(2,1)S(1)}) custom-call(s32[3]{0:T(128)S(1)} %pad_add_fusion.place, f32[2,2,4,128]{3,2,1,0:T(4,128)S(1)} %copy-done, s32[2,4]{1,0:T(2,128)S(1)} %copy-done.1, f32[2,4,128]{2,1,0:T(4,128)S(1)} %copy-done.2), custom_call_target="tpu_custom_call" | custom-call | flops 4000000 | bytes 65536 | tf_op jit(solution)/shard_map/pallas_call | solution.py:30
  2.4 0.6 %collective-permute-start = (f32[7,8,128]{2,1,0:T(8,128)S(1)}, f32[7,8,128]{2,1,0:T(8,128)S(1)}, u32[]{:S(2)}, u32[]{:S(2)}) collective-permute-start(f32[7,8,128]{2,1,0:T(8,128)S(1)} %get-tuple-element.5.own), channel_id=1, source_target_pairs={{0,4},{1,5},{2,6},{3,7},{4,0},{5,1},{6,2},{7,3},{8,12},{9,13},{10,... | collective-permute-start | bytes 86024 | tf_op jit(solution)/shard_map/ppermute | solution.py:372
  3.0 0.8 %collective-permute-done.partner = f32[7,8,128]{2,1,0:T(8,128)S(1)} collective-permute-done((f32[7,8,128]{2,1,0:T(8,128)S(1)}, f32[7,8,128]{2,1,0:T(8,128)S(1)}, u32[]{:S(2)}, u32[]{:S(2)}) %collective-permute-start) | collective-permute-done | bytes 28704 | tf_op jit(solution)/shard_map/ppermute | solution.py:372
  3.8 2.7 %collective-permute-start.1 = (f32[7,8,128]{2,1,0:T(8,128)S(1)}, f32[7,8,128]{2,1,0:T(8,128)S(1)}, u32[]{:S(2)}, u32[]{:S(2)}) collective-permute-start(f32[7,8,128]{2,1,0:T(8,128)S(1)} %maximum_maximum_fusion), channel_id=1, source_target_pairs={{0,12},{1,13},{2,14},{3,15},{4,8},{5,9},{6,10},{7,11},{8,4},{9,5},... | collective-permute-start | bytes 86024 | tf_op jit(solution)/shard_map/ppermute | solution.py:372
  6.5 1.6 %collective-permute-done.1 = f32[7,8,128]{2,1,0:T(8,128)S(1)} collective-permute-done((f32[7,8,128]{2,1,0:T(8,128)S(1)}, f32[7,8,128]{2,1,0:T(8,128)S(1)}, u32[]{:S(2)}, u32[]{:S(2)}) %collective-permute-start.1) | collective-permute-done | bytes 28704 | tf_op jit(solution)/shard_map/ppermute | solution.py:372
  8.1 1.8 %collective-permute-start.2 = (f32[7,8,128]{2,1,0:T(8,128)S(1)}, f32[7,8,128]{2,1,0:T(8,128)S(1)}, u32[]{:S(2)}, u32[]{:S(2)}) collective-permute-start(f32[7,8,128]{2,1,0:T(8,128)S(1)} %pad_maximum_fusion), channel_id=1, source_target_pairs={{0,20},{1,21},{2,22},{3,23},{4,16},{5,17},{6,18},{7,19},{8,28},{9,... | collective-permute-start | bytes 86024 | tf_op jit(solution)/shard_map/ppermute | solution.py:372
  9.9 1.6 %collective-permute-done.2 = f32[7,8,128]{2,1,0:T(8,128)S(1)} collective-permute-done((f32[7,8,128]{2,1,0:T(8,128)S(1)}, f32[7,8,128]{2,1,0:T(8,128)S(1)}, u32[]{:S(2)}, u32[]{:S(2)}) %collective-permute-start.2) | collective-permute-done | bytes 28704 | tf_op jit(solution)/shard_map/ppermute | solution.py:372
  11.5 0.1 fusion
  11.6 0.6 %shard_map.51.packed = f32[13,8,128]{2,1,0:T(8,128)S(1)} custom-call(s32[3]{0:T(128)S(1)} %pad_add_fusion.place, f32[7,8,128]{2,1,0:T(8,128)S(1)} %get-tuple-element.5.own, f32[7,8,128]{2,1,0:T(8,128)S(1)} %collective-permute-done.partner, f32[7,8,128]{2,1,0:T(8,128)S(1)} %pad_maximum_fusion.1.ring), custom_call_target="tpu_custom_call" | custom-call | flops 100000 | bytes 65536 | tf_op jit(solution)/shard_map/pallas_call | solution.py:30
  12.1 1.9 %collective-permute-start.3 = (f32[13,8,128]{2,1,0:T(8,128)S(1)}, f32[13,8,128]{2,1,0:T(8,128)S(1)}, u32[]{:S(2)}, u32[]{:S(2)}) collective-permute-start(f32[13,8,128]{2,1,0:T(8,128)S(1)} %shard_map.51.packed), channel_id=1, source_target_pairs={{0,5},{1,4},{2,7},{3,6},{4,1},{5,0},{6,3},{7,2},{8,13},{9,12},{10,... | collective-permute-start | bytes 159752 | tf_op jit(solution)/shard_map/ppermute | solution.py:372
  14.0 1.9 %collective-permute-done.3 = f32[13,8,128]{2,1,0:T(8,128)S(1)} collective-permute-done((f32[13,8,128]{2,1,0:T(8,128)S(1)}, f32[13,8,128]{2,1,0:T(8,128)S(1)}, u32[]{:S(2)}, u32[]{:S(2)}) %collective-permute-start.3) | collective-permute-done | bytes 53280 | tf_op jit(solution)/shard_map/ppermute | solution.py:372
  15.9 3.0 %collective-permute-start.4 = (f32[7,8,128]{2,1,0:T(8,128)S(1)}, f32[7,8,128]{2,1,0:T(8,128)S(1)}, u32[]{:S(2)}, u32[]{:S(2)}) collective-permute-start(f32[7,8,128]{2,1,0:T(8,128)S(1)} %pad_maximum_fusion.2), channel_id=1, source_target_pairs={{0,6},{1,7},{2,4},{3,5},{4,2},{5,3},{6,0},{7,1},{8,14},{9,15},{10,... | collective-permute-start | bytes 86024 | tf_op jit(solution)/shard_map/ppermute | solution.py:372
  18.9 1.0 %shard_map.52.near_a = f32[2,8,128]{2,1,0:T(8,128)S(1)} custom-call(f32[7,8,128]{2,1,0:T(8,128)S(1)} %get-tuple-element.5.own), custom_call_target="tpu_custom_call" | custom-call | flops 4000000 | bytes 65536 | tf_op jit(solution)/shard_map/pallas_call | solution.py:30
  19.8 1.4 %shard_map.53.near_b = f32[2,8,128]{2,1,0:T(8,128)S(1)} custom-call(f32[7,8,128]{2,1,0:T(8,128)S(1)} %get-tuple-element.5.own), custom_call_target="tpu_custom_call" | custom-call | flops 9000000 | bytes 65536 | tf_op jit(solution)/shard_map/pallas_call | solution.py:30
  21.3 2.5 %shard_map.54.near_c = f32[2,8,128]{2,1,0:T(8,128)S(1)} custom-call(s32[3]{0:T(128)S(1)} %pad_add_fusion.place, f32[7,8,128]{2,1,0:T(8,128)S(1)} %get-tuple-element.5.own, f32[7,8,128]{2,1,0:T(8,128)S(1)} %collective-permute-done.partner), custom_call_target="tpu_custom_call" | custom-call | flops 9000000 | bytes 65536 | tf_op jit(solution)/shard_map/pallas_call | solution.py:30
  23.8 1.6 %shard_map.55.near_d = f32[2,8,128]{2,1,0:T(8,128)S(1)} custom-call(s32[3]{0:T(128)S(1)} %pad_add_fusion.place, f32[7,8,128]{2,1,0:T(8,128)S(1)} %get-tuple-element.5.own, f32[13,8,128]{2,1,0:T(8,128)S(1)} %shard_map.51.packed), custom_call_target="tpu_custom_call" | custom-call | flops 5000000 | bytes 65536 | tf_op jit(solution)/shard_map/pallas_call | solution.py:30
  25.4 1.6 %shard_map.56.near_e = f32[2,8,128]{2,1,0:T(8,128)S(1)} custom-call(s32[3]{0:T(128)S(1)} %pad_add_fusion.place, f32[7,8,128]{2,1,0:T(8,128)S(1)} %get-tuple-element.5.own, f32[3,8,128]{2,1,0:T(8,128)S(1)} %get-tuple-element.8.close), custom_call_target="tpu_custom_call" | custom-call | flops 3000000 | bytes 65536 | tf_op jit(solution)/shard_map/pallas_call | solution.py:30
  27.0 0.0 collective-permute-done.4
  27.0 2.4 %shard_map.57 = (f32[2,2,4,128]{3,2,1,0:T(4,128)}, f32[2,2,4,128]{3,2,1,0:T(4,128)}) custom-call(s32[3]{0:T(128)S(1)} %pad_add_fusion.place, f32[2,2,4,128]{3,2,1,0:T(4,128)S(1)} %copy-done, s32[2,4]{1,0:T(2,128)S(1)} %copy-done.1, f32[7,8,128]{2,1,0:T(8,128)S(1)} %get-tuple-element.5.own, f32[64,1024]{1,0:T(8,128)S(1)} %get-tuple-element.6.x_table, ...), custom_call_target="tpu_custom_call" | custom-call | flops 4000000 | bytes 65536 | tf_op jit(solution)/shard_map/pallas_call | solution.py:30
  (21 shorter events, 0.1 us)
Async XLA Ops:
  0.6 0.7 %copy-start = (f32[2,2,4,128]{3,2,1,0:T(4,128)S(1)}, f32[2,2,4,128]{3,2,1,0:T(4,128)}, u32[]{:S(2)}) copy-start(f32[2,2,4,128]{3,2,1,0:T(4,128)} %offsets.3) | copy-start | bytes 24580
  0.7 0.7 %copy-start.2 = (f32[2,4,128]{2,1,0:T(4,128)S(1)}, f32[2,4,128]{2,1,0:T(4,128)}, u32[]{:S(2)}) copy-start(f32[2,4,128]{2,1,0:T(4,128)} %circ.1) | copy-start | bytes 12292
  0.7 0.7 %copy-start.1 = (s32[2,4]{1,0:T(2,128)S(1)}, s32[2,4]{1,0:T(2,128)}, u32[]{:S(2)}) copy-start(s32[2,4]{1,0:T(2,128)} %counts.3) | copy-start | bytes 100
  2.4 1.4 %collective-permute-start = (f32[7,8,128]{2,1,0:T(8,128)S(1)}, f32[7,8,128]{2,1,0:T(8,128)S(1)}, u32[]{:S(2)}, u32[]{:S(2)}) collective-permute-start(f32[7,8,128]{2,1,0:T(8,128)S(1)} %get-tuple-element.5.own), channel_id=1, source_target_pairs={{0,4},{1,5},{2,6},{3,7},{4,0},{5,1},{6,2},{7,3},{8,12},{9,13},{10,... | collective-permute-start | bytes 86024 | tf_op jit(solution)/shard_map/ppermute | solution.py:372
  3.8 4.2 %collective-permute-start.1 = (f32[7,8,128]{2,1,0:T(8,128)S(1)}, f32[7,8,128]{2,1,0:T(8,128)S(1)}, u32[]{:S(2)}, u32[]{:S(2)}) collective-permute-start(f32[7,8,128]{2,1,0:T(8,128)S(1)} %maximum_maximum_fusion), channel_id=1, source_target_pairs={{0,12},{1,13},{2,14},{3,15},{4,8},{5,9},{6,10},{7,11},{8,4},{9,5},... | collective-permute-start | bytes 86024 | tf_op jit(solution)/shard_map/ppermute | solution.py:372
  8.1 3.4 %collective-permute-start.2 = (f32[7,8,128]{2,1,0:T(8,128)S(1)}, f32[7,8,128]{2,1,0:T(8,128)S(1)}, u32[]{:S(2)}, u32[]{:S(2)}) collective-permute-start(f32[7,8,128]{2,1,0:T(8,128)S(1)} %pad_maximum_fusion), channel_id=1, source_target_pairs={{0,20},{1,21},{2,22},{3,23},{4,16},{5,17},{6,18},{7,19},{8,28},{9,... | collective-permute-start | bytes 86024 | tf_op jit(solution)/shard_map/ppermute | solution.py:372
  12.1 3.7 %collective-permute-start.3 = (f32[13,8,128]{2,1,0:T(8,128)S(1)}, f32[13,8,128]{2,1,0:T(8,128)S(1)}, u32[]{:S(2)}, u32[]{:S(2)}) collective-permute-start(f32[13,8,128]{2,1,0:T(8,128)S(1)} %shard_map.51.packed), channel_id=1, source_target_pairs={{0,5},{1,4},{2,7},{3,6},{4,1},{5,0},{6,3},{7,2},{8,13},{9,12},{10,... | collective-permute-start | bytes 159752 | tf_op jit(solution)/shard_map/ppermute | solution.py:372
  15.9 11.1 %collective-permute-start.4 = (f32[7,8,128]{2,1,0:T(8,128)S(1)}, f32[7,8,128]{2,1,0:T(8,128)S(1)}, u32[]{:S(2)}, u32[]{:S(2)}) collective-permute-start(f32[7,8,128]{2,1,0:T(8,128)S(1)} %pad_maximum_fusion.2), channel_id=1, source_target_pairs={{0,6},{1,7},{2,4},{3,5},{4,2},{5,3},{6,0},{7,1},{8,14},{9,15},{10,... | collective-permute-start | bytes 86024 | tf_op jit(solution)/shard_map/ppermute | solution.py:372

commit v2 on v1

--- a/solution.py
+++ b/solution.py
@@ -20,35 +20,25 @@
 floor_term = smooth * unit * unit
 
 VMEM = pl.BlockSpec(memory_space=pltpu.VMEM)
-SMEM = pl.BlockSpec(memory_space=pltpu.SMEM)
 PARAMS = pltpu.CompilerParams(vmem_limit_bytes=8 * 1024 * 1024)
 
 
+def position():
+    tx = lax.axis_index("tx")
+    return tx, lax.axis_index("ty"), lax.rem(tx, 2)
+
+
 def call(body, out_shapes, scratch, flops, *args):
-    specs = [SMEM if a.dtype == jnp.int32 else VMEM for a in args]
     outs = [jax.ShapeDtypeStruct(s, d) for s, d in out_shapes]
     return pl.pallas_call(
         body,
         out_shape=outs,
-        in_specs=specs,
+        in_specs=[VMEM] * len(args),
         out_specs=[VMEM] * len(outs),
         scratch_shapes=scratch,
         compiler_params=PARAMS,
         cost_estimate=pl.CostEstimate(flops=flops, bytes_accessed=65536, transcendentals=0),
     )(*args)
-
-
-def cell_rows(ref, rows):
-    return jnp.concatenate([ref[r] for r in range(rows)], axis=0)
-
-
-def count_grid(counts_ref, rows, cols, shape):
-    cell = lax.broadcasted_iota(jnp.int32, shape, 0)
-    limit = jnp.zeros(shape, jnp.int32)
-    for r in range(rows):
-        for c in range(cols):
-            limit = jnp.where(cell == r * cols + c, counts_ref[r, c], limit)
-    return lax.broadcasted_iota(jnp.int32, shape, 1) < limit
 
 
 def unit_circle(turn):
@@ -80,20 +70,21 @@
 
 
 def moments_kernel(
-    rows, cols, cell_count, place, offsets, counts, circ, own, x_table, y_table, powers, weighted
+    rows, cols, cell_count, slot_state, own, kept, x_table, y_table, powers, weighted
 ):
     cells = rows * cols
-    slots = circ.shape[2]
+    slots = slot_state.shape[3]
     shape = (cells, slots)
+    place = position()
     cell = lax.broadcasted_iota(jnp.int32, shape, 0)
     row_in = jnp.zeros(shape, jnp.int32)
     for r in range(1, rows):
         row_in = jnp.where(cell >= r * cols, r, row_in)
     col_in = cell - row_in * cols
-    live = count_grid(counts, rows, cols, shape)
-    strength = jnp.where(live, cell_rows(circ, rows), 0.0)
-    off_x = cell_rows(offsets.at[0], rows)
-    off_y = cell_rows(offsets.at[1], rows)
+    for part in range(4):
+        for r in range(rows):
+            kept[part, pl.ds(r * cols, cols), :] = slot_state[part, r]
+    off_x, off_y, strength = kept[0], kept[1], kept[2]
     x_turn = ((place[1] * cols + col_in).astype(jnp.float32) + off_x) / cell_count
     y_turn = ((place[0] * rows + row_in).astype(jnp.float32) + off_y) / cell_count
     own[4] = unit * (col_in.astype(jnp.float32) + off_x)
@@ -178,10 +169,18 @@
         return tuple(totals)
 
     zero = jnp.zeros((8, slots), jnp.float32)
-    totals = (zero,) * (2 * len(targets))
-    totals = lax.fori_loop(
-        0, slots // 16, lambda k, held: step(2 * k + 1, step(2 * k, held)), totals
-    )
+    pairs = sum(len(reached) for reached in links)
+    chunks = slots // 8
+    group = 1
+    while group * 2 * pairs <= 48 and chunks % (group * 2) == 0:
+        group *= 2
+
+    def grouped(k, totals):
+        for u in range(group):
+            totals = step(k * group + u, totals)
+        return totals
+
+    totals = lax.fori_loop(0, chunks // group, grouped, (zero,) * (2 * len(targets)))
     return [jnp.sum(total, axis=0, keepdims=True) for total in totals]
 
 
@@ -248,25 +247,41 @@
             near[part, at, :] = near[part, at, :] + sums[2 * r + part]
 
 
-def near_partner_kernel(rows, cols, cells, place, own, partner, near, turned):
+def near_partner_kernel(rows, cols, cells, own, partner, near, turned):
+    place = position()
     near[...] = jnp.zeros_like(near)
     near_local(rows, cols, own, cells, near, turned)
     near_rows(rows, cols, own, partner, 4, place[2], near, turned)
 
 
-def near_ring_kernel(rows, cols, place, own, packed, near, turned):
+def near_ring_kernel(rows, cols, own, ring, near, turned):
+    place = position()
     near[...] = jnp.zeros_like(near)
-    near_rows(rows, cols, own, packed, 10, 1 - place[2], near, turned)
-
-
-def near_close_kernel(rows, cols, place, own, close, near, turned):
+    near_rows(rows, cols, own, ring, 0, 1 - place[2], near, turned)
+
+
+def near_close_kernel(rows, cols, cell_count, own, close, near, weights, turned):
+    shape = (HALF, 2 * MODES)
+    lane = lax.broadcasted_iota(jnp.int32, shape, 1)
+    m = lax.broadcasted_iota(jnp.int32, shape, 0).astype(jnp.float32)
+    n = (lane & (HALF - 1)).astype(jnp.float32)
+    square = (two_pi * two_pi) * (m * m + n * n)
+    keep = square > 0.0
+    safe = jnp.where(keep, square, 1.0)
+    damping = jnp.where(keep, jnp.exp(-safe / (6.25 * cell_count * cell_count)) / safe, 0.0)
+    damping = damping * (4.0 * two_pi)
+    u_weight = damping * n * jnp.where(m == 0.0, 0.5, 1.0)
+    v_weight = damping * m * jnp.where(n == 0.0, 0.5, 1.0)
+    weights[0] = u_weight
+    weights[1] = v_weight
+    place = position()
     near[...] = jnp.zeros_like(near)
     right = 1 - lax.rem(place[1], 2)
     near_cols(rows, cols, own, close, 0, place[2], right, near, turned)
 
 
-def pack_kernel(rows, cols, place, own, partner, ring, packed):
-    core = place[2]
+def pack_kernel(rows, cols, own, partner, ring, packed, ring_out):
+    core = position()[2]
     packed[4:10] = jnp.zeros((6,) + packed.shape[1:], jnp.float32)
     packed[0:4] = ring[0:4]
     for edge, col in ((0, 0), (1, cols - 1)):
@@ -278,33 +293,25 @@
                 packed[at, pl.ds(1 + rows * core + r, 1), :] = own[4 + part, cell, :]
                 packed[at, pl.ds(1 + rows * (1 - core) + r, 1), :] = partner[4 + part, cell, :]
             packed[at, pl.ds(1 + 2 * rows, 1), :] = ring[4 + part, pl.ds(col, 1), :]
-    packed[10:13] = ring[4:7]
+    ring_out[...] = ring[4:7]
 
 
 def final_kernel(
-    rows, cols, cell_count, place, offsets, counts, own, x_table, y_table, last,
-    near_a, near_b, near_c, near_d, near_e, velocity, moved, near, far, turned,
+    rows, cols, kept, own, x_table, y_table, last,
+    near_a, near_b, near_c, near_d, near_e, weights, velocity, moved, near, far, turned,
 ):
     cells = rows * cols
     slots = own.shape[2]
+    place = position()
     core = place[2]
     shape = (HALF, 2 * MODES)
     lane = lax.broadcasted_iota(jnp.int32, shape, 1)
-    m = lax.broadcasted_iota(jnp.int32, shape, 0).astype(jnp.float32)
-    n = (lane & (HALF - 1)).astype(jnp.float32)
-    square = (two_pi * two_pi) * (m * m + n * n)
-    keep = square > 0.0
-    safe = jnp.where(keep, square, 1.0)
-    damping = jnp.where(keep, jnp.exp(-safe / (6.25 * cell_count * cell_count)) / safe, 0.0)
-    damping = damping * (4.0 * two_pi)
-    u_weight = damping * n * jnp.where(m == 0.0, 0.5, 1.0)
-    v_weight = damping * m * jnp.where(n == 0.0, 0.5, 1.0)
     total = last[0:4].reshape(shape)
     y_odd = (lane & HALF) != 0
     swapped = jnp.where(y_odd, -pltpu.roll(total, HALF, 1), pltpu.roll(total, 2 * MODES - HALF, 1))
-    u_part = u_weight * swapped
+    u_part = weights[0] * swapped
     crossed = pltpu.roll(total, MODES, 1)
-    v_part = v_weight * jnp.where(lane < MODES, -crossed, crossed)
+    v_part = weights[1] * jnp.where(lane < MODES, -crossed, crossed)
     left = []
     for part in (u_part, v_part):
         other = pltpu.roll(part, MODES, 1)
@@ -323,13 +330,13 @@
         far[1, pl.ds(i, 1), :] = jnp.sum(terms[MODES:, lanes] * wave, axis=0, keepdims=True)
     near[...] = (near_a[...] + near_b[...]) + (near_c[...] + near_d[...]) + near_e[...]
     near_cols(rows, cols, own, last, 4, core, lax.rem(place[1], 2), near, turned)
-    live = count_grid(counts, rows, cols, (cells, slots))
+    live = kept[3] > 0.5
     for part in range(2):
         value = jnp.where(live, near[part] + far[part], 0.0)
+        after = kept[part] + section_step * value
         for r in range(rows):
-            piece = value[r * cols : (r + 1) * cols]
-            velocity[part, r] = piece
-            moved[part, r] = offsets[part, r] + section_step * piece
+            velocity[part, r] = value[r * cols : (r + 1) * cols]
+            moved[part, r] = after[r * cols : (r + 1) * cols]
 
 
 def far_item(items, index):
@@ -350,17 +357,28 @@
     cell_count = rows * tx_size
     tx, ty = lax.axis_index("tx"), lax.axis_index("ty")
     core, chip = tx % 2, tx // 2
-    place = jnp.stack([tx, ty, core]).astype(jnp.int32)
     f32, bf16 = jnp.float32, jnp.bfloat16
     turned = [pltpu.VMEM((slots, 128), f32)]
     near_shape = [((2, cells, slots), f32)]
 
-    own, x_table, y_table = call(
+    live = lax.broadcasted_iota(jnp.int32, circ.shape, 2) < counts[:, :, None]
+    slot_state = jnp.stack(
+        [offsets[0], offsets[1], jnp.where(live, circ, 0.0), jnp.where(live, 1.0, 0.0)]
+    )
+    own, kept, x_table, y_table = call(
         functools.partial(moments_kernel, rows, cols, cell_count),
-        [((7, cells, slots), f32), ((MODES, cells * slots), f32), ((2 * MODES, cells * slots), bf16)],
-        [pltpu.VMEM((2, 5, 3, cells, slots), f32), pltpu.VMEM((2 * MODES, cells * slots), bf16)],
+        [
+            ((7, cells, slots), f32),
+            ((4, cells, slots), f32),
+            ((MODES, cells * slots), f32),
+            ((2 * MODES, cells * slots), bf16),
+        ],
+        [
+            pltpu.VMEM((2, 5, 3, cells, slots), f32),
+            pltpu.VMEM((2 * MODES, cells * slots), bf16),
+        ],
         4_000_000,
-        place, offsets, counts, circ,
+        slot_state,
     )
 
     def swap(message, chip_bit, column_bit):
@@ -396,7 +414,7 @@
     )
     near_c = near_call(
         functools.partial(near_partner_kernel, rows, cols, whole[3 * third :]), 9_000_000,
-        place, own, partner,
+        own, partner,
     )
     slot_of = lax.broadcasted_iota(jnp.int32, (3, 2 * cols, slots), 1)
     below = slot_of < cols
@@ -405,14 +423,13 @@
     shift = jnp.where(below, 2.0 * rows * unit, -2.0 * rows * unit)
     which = lax.broadcasted_iota(jnp.int32, (3, 2 * cols, slots), 0)
     ring = ring + jnp.where(which == 1, shift, 0.0)
-    (packed,) = call(
-        functools.partial(pack_kernel, rows, cols), [((13, cells, slots), f32)], [], 100_000,
-        place, own, partner, jnp.concatenate([total, ring], axis=0),
+    packed, ring = call(
+        functools.partial(pack_kernel, rows, cols),
+        [((10, cells, slots), f32), ((3, 2 * cols, slots), f32)], [], 100_000,
+        own, partner, jnp.concatenate([total, ring], axis=0),
     )
     got = swap(packed, 0, 1)
-    near_d = near_call(
-        functools.partial(near_ring_kernel, rows, cols), 5_000_000, place, own, packed
-    )
+    near_d = near_call(functools.partial(near_ring_kernel, rows, cols), 5_000_000, own, ring)
     total = packed[0:4] + got[0:4]
     close = jnp.where(ty % 2 == 0, got[4:7], got[7:10])
     items = [None, jnp.where(ty % 2 == 0, got[7:10], got[4:7])]
@@ -423,19 +440,21 @@
         total = total + got[0:4]
         items.append(got[4:7])
         bit *= 2
-    near_e = near_call(
-        functools.partial(near_close_kernel, rows, cols), 3_000_000, place, own, close
+    near_e, weights = call(
+        functools.partial(near_close_kernel, rows, cols, cell_count),
+        near_shape + [((2, HALF, 2 * MODES), f32)], turned, 3_000_000,
+        own, close,
     )
     distant = far_item(items, ty) if ty_size > 2 else items[1]
     last = jnp.concatenate([total, distant], axis=0)
     return tuple(
         call(
-            functools.partial(final_kernel, rows, cols, cell_count),
+            functools.partial(final_kernel, rows, cols),
             [(offsets.shape, f32)] * 2,
             [pltpu.VMEM((2, cells, slots), f32), pltpu.VMEM((2, cells, slots), f32)] + turned,
             4_000_000,
-            place, offsets, counts, own, x_table, y_table, last,
-            near_a, near_b, near_c, near_d, near_e,
+            kept, own, x_table, y_table, last,
+            near_a, near_b, near_c, near_d, near_e, weights,
         )
     )
 

time: 29.7 us -> 24.2 us (0.81)
  Pallas kernels: 12.1 us -> 6.76 us
  other arithmetic: 0.23 us -> 1.03 us
  local copies, waits for them, and re-layouts: 0.61 us -> 0.02 us
    pallas_call x8, Pallas kernels: 12.1 us -> 6.76 us  [call(): pl.pallas_call(body, out_shape=outs, in_specs=[VMEM] * len(args), out_spe...]
    select_n x0 -> x1, other arithmetic: none -> 0.79 us  [per_device(): jnp.where(live, 1.0, 0.0)]
    unnamed x6, local copies, waits for them, and re-layouts: 0.6 us -> 0.01 us
  transfers between devices with their start and end apart: 5 -> 5, of which waited for: 4 -> 4; matrix products, arithmetic and copies ran while one was open for 0% -> 0% of each run, Pallas kernels for 27% -> 20%
where the time goes in v2:
time: 24.2 us; the launch traced here: 24.1 us
  starting transfers between devices  9.82 us (41%)
  Pallas kernels  6.76 us (28%)
  waiting for transfers between devices  5.64 us (23%)
  other arithmetic  1.03 us (4%)
  between operations  0.79 us (3%)
    ppermute x5, starting transfers between devices, swap(): return lax.ppermute(message, ('tx', 'ty'), pairs)  9.82 us
    pallas_call x8, Pallas kernels, call(): pl.pallas_call(body, out_shape=outs, in_specs=[VMEM] * len(args), out_spe...  6.76 us
    ppermute x5, waiting for transfers between devices, swap(): return lax.ppermute(message, ('tx', 'ty'), pairs)  5.64 us
    select_n x1, other arithmetic, per_device(): jnp.where(live, 1.0, 0.0)  0.79 us
  transfers between devices with their start and end apart: 5, of which 4 were waited for; matrix products, arithmetic and copies ran while one was open for 0% of the time, Pallas kernels for 20%

profile of v2, /device:TPU:0, one launch (start us, length us, event | category | flops | bytes accessed | tf_op | source)
XLA Modules:
  0.0 24.1 jit_solution(11127704724592161445)
XLA Ops:
  0.6 0.0 copy-start.1
  0.6 0.0 copy-start.2
  0.6 0.0 copy-start
  0.7 0.8 %fusion.1 = f32[1,2,4,128]{3,2,1,0:T(4,128)S(1)} fusion(s32[2,4]{1,0:T(2,128)} %param.5), kind=kLoop, calls=%fused_computation.20 | loop fusion | flops 2048 | bytes 4128 | tf_op jit(solution)/shard_map/jit(_where)/select_n | solution.py:366
  1.5 0.0 copy-done.2
  1.5 0.1 select_bitcast_fusion
  1.5 0.5 %shard_map.50 = (f32[7,8,128]{2,1,0:T(8,128)S(1)}, f32[4,8,128]{2,1,0:T(8,128)S(1)}, f32[64,1024]{1,0:T(8,128)S(1)}, bf16[128,1024]{1,0:T(8,128)(2,1)S(1)}) custom-call(f32[4,2,4,128]{3,2,1,0:T(4,128)S(1)} %pad_maximum_fusion.4.slot_state), custom_call_target="tpu_custom_call" | custom-call | flops 4000000 | bytes 65536 | tf_op jit(solution)/shard_map/pallas_call | solution.py:33
  2.0 0.6 %collective-permute-start = (f32[7,8,128]{2,1,0:T(8,128)S(1)}, f32[7,8,128]{2,1,0:T(8,128)S(1)}, u32[]{:S(2)}, u32[]{:S(2)}) collective-permute-start(f32[7,8,128]{2,1,0:T(8,128)S(1)} %get-tuple-element.11.own), channel_id=1, source_target_pairs={{0,4},{1,5},{2,6},{3,7},{4,0},{5,1},{6,2},{7,3},{8,12},{9,13},{10,... | collective-permute-start | bytes 86024 | tf_op jit(solution)/shard_map/ppermute | solution.py:390
  2.6 0.8 %collective-permute-done.partner = f32[7,8,128]{2,1,0:T(8,128)S(1)} collective-permute-done((f32[7,8,128]{2,1,0:T(8,128)S(1)}, f32[7,8,128]{2,1,0:T(8,128)S(1)}, u32[]{:S(2)}, u32[]{:S(2)}) %collective-permute-start) | collective-permute-done | bytes 28704 | tf_op jit(solution)/shard_map/ppermute | solution.py:390
  3.5 2.7 %collective-permute-start.1 = (f32[7,8,128]{2,1,0:T(8,128)S(1)}, f32[7,8,128]{2,1,0:T(8,128)S(1)}, u32[]{:S(2)}, u32[]{:S(2)}) collective-permute-start(f32[7,8,128]{2,1,0:T(8,128)S(1)} %maximum_maximum_fusion), channel_id=1, source_target_pairs={{0,12},{1,13},{2,14},{3,15},{4,8},{5,9},{6,10},{7,11},{8,4},{9,5},... | collective-permute-start | bytes 86024 | tf_op jit(solution)/shard_map/ppermute | solution.py:390
  6.2 1.6 %collective-permute-done.1 = f32[7,8,128]{2,1,0:T(8,128)S(1)} collective-permute-done((f32[7,8,128]{2,1,0:T(8,128)S(1)}, f32[7,8,128]{2,1,0:T(8,128)S(1)}, u32[]{:S(2)}, u32[]{:S(2)}) %collective-permute-start.1) | collective-permute-done | bytes 28704 | tf_op jit(solution)/shard_map/ppermute | solution.py:390
  7.7 1.8 %collective-permute-start.2 = (f32[7,8,128]{2,1,0:T(8,128)S(1)}, f32[7,8,128]{2,1,0:T(8,128)S(1)}, u32[]{:S(2)}, u32[]{:S(2)}) collective-permute-start(f32[7,8,128]{2,1,0:T(8,128)S(1)} %pad_maximum_fusion), channel_id=1, source_target_pairs={{0,20},{1,21},{2,22},{3,23},{4,16},{5,17},{6,18},{7,19},{8,28},{9,... | collective-permute-start | bytes 86024 | tf_op jit(solution)/shard_map/ppermute | solution.py:390
  9.6 1.6 %collective-permute-done.2 = f32[7,8,128]{2,1,0:T(8,128)S(1)} collective-permute-done((f32[7,8,128]{2,1,0:T(8,128)S(1)}, f32[7,8,128]{2,1,0:T(8,128)S(1)}, u32[]{:S(2)}, u32[]{:S(2)}) %collective-permute-start.2) | collective-permute-done | bytes 28704 | tf_op jit(solution)/shard_map/ppermute | solution.py:390
  11.1 0.1 fusion
  11.2 1.9 %collective-permute-start.3 = (f32[10,8,128]{2,1,0:T(8,128)S(1)}, f32[10,8,128]{2,1,0:T(8,128)S(1)}, u32[]{:S(2)}, u32[]{:S(2)}) collective-permute-start(f32[10,8,128]{2,1,0:T(8,128)S(1)} %get-tuple-element.14), channel_id=1, source_target_pairs={{0,5},{1,4},{2,7},{3,6},{4,1},{5,0},{6,3},{7,2},{8,13},{9,12},{10,... | collective-permute-start | bytes 122888 | tf_op jit(solution)/shard_map/ppermute | solution.py:390
  13.1 1.7 %collective-permute-done.3 = f32[10,8,128]{2,1,0:T(8,128)S(1)} collective-permute-done((f32[10,8,128]{2,1,0:T(8,128)S(1)}, f32[10,8,128]{2,1,0:T(8,128)S(1)}, u32[]{:S(2)}, u32[]{:S(2)}) %collective-permute-start.3) | collective-permute-done | bytes 40992 | tf_op jit(solution)/shard_map/ppermute | solution.py:390
  14.8 2.9 %collective-permute-start.4 = (f32[7,8,128]{2,1,0:T(8,128)S(1)}, f32[7,8,128]{2,1,0:T(8,128)S(1)}, u32[]{:S(2)}, u32[]{:S(2)}) collective-permute-start(f32[7,8,128]{2,1,0:T(8,128)S(1)} %pad_maximum_fusion.2), channel_id=1, source_target_pairs={{0,6},{1,7},{2,4},{3,5},{4,2},{5,3},{6,0},{7,1},{8,14},{9,15},{10,... | collective-permute-start | bytes 86024 | tf_op jit(solution)/shard_map/ppermute | solution.py:390
  17.7 0.6 %shard_map.52.near_a = f32[2,8,128]{2,1,0:T(8,128)S(1)} custom-call(f32[7,8,128]{2,1,0:T(8,128)S(1)} %get-tuple-element.11.own), custom_call_target="tpu_custom_call" | custom-call | flops 4000000 | bytes 65536 | tf_op jit(solution)/shard_map/pallas_call | solution.py:33
  18.4 1.4 %shard_map.53.near_b = f32[2,8,128]{2,1,0:T(8,128)S(1)} custom-call(f32[7,8,128]{2,1,0:T(8,128)S(1)} %get-tuple-element.11.own), custom_call_target="tpu_custom_call" | custom-call | flops 9000000 | bytes 65536 | tf_op jit(solution)/shard_map/pallas_call | solution.py:33
  19.8 1.4 %shard_map.54.near_c = f32[2,8,128]{2,1,0:T(8,128)S(1)} custom-call(f32[7,8,128]{2,1,0:T(8,128)S(1)} %get-tuple-element.11.own, f32[7,8,128]{2,1,0:T(8,128)S(1)} %collective-permute-done.partner), custom_call_target="tpu_custom_call" | custom-call | flops 9000000 | bytes 65536 | tf_op jit(solution)/shard_map/pallas_call | solution.py:33
  21.2 0.8 %shard_map.55.near_d = f32[2,8,128]{2,1,0:T(8,128)S(1)} custom-call(f32[7,8,128]{2,1,0:T(8,128)S(1)} %get-tuple-element.11.own, f32[3,8,128]{2,1,0:T(8,128)S(1)} %get-tuple-element.15.ring), custom_call_target="tpu_custom_call" | custom-call | flops 5000000 | bytes 65536 | tf_op jit(solution)/shard_map/pallas_call | solution.py:33
  22.0 0.6 %shard_map.56 = (f32[2,8,128]{2,1,0:T(8,128)S(1)}, f32[2,32,128]{2,1,0:T(8,128)S(1)}) custom-call(f32[7,8,128]{2,1,0:T(8,128)S(1)} %get-tuple-element.11.own, f32[3,8,128]{2,1,0:T(8,128)S(1)} %get-tuple-element.18.close), custom_call_target="tpu_custom_call" | custom-call | flops 3000000 | bytes 65536 | tf_op jit(solution)/shard_map/pallas_call | solution.py:33
  22.6 0.0 collective-permute-done.4
  22.6 1.4 %shard_map.57 = (f32[2,2,4,128]{3,2,1,0:T(4,128)}, f32[2,2,4,128]{3,2,1,0:T(4,128)}) custom-call(f32[4,8,128]{2,1,0:T(8,128)S(1)} %get-tuple-element.10.kept, f32[7,8,128]{2,1,0:T(8,128)S(1)} %get-tuple-element.11.own, f32[64,1024]{1,0:T(8,128)S(1)} %get-tuple-element.12.x_table, bf16[128,1024]{1,0:T(8,128)(2,1)S(1)} %get-tuple-element.13.y_table, ...), custom_call_target="tpu_custom_call" | custom-call | flops 4000000 | bytes 65536 | tf_op jit(solution)/shard_map/pallas_call | solution.py:33
  (23 shorter events, 0.1 us)
Async XLA Ops:
  0.6 0.8 %copy-start.1 = (s32[2,4]{1,0:T(2,128)S(1)}, s32[2,4]{1,0:T(2,128)}, u32[]{:S(2)}) copy-start(s32[2,4]{1,0:T(2,128)} %param.5) | copy-start | bytes 100
  0.6 0.8 %copy-start.2 = (f32[2,4,128]{2,1,0:T(4,128)S(1)}, f32[2,4,128]{2,1,0:T(4,128)}, u32[]{:S(2)}) copy-start(f32[2,4,128]{2,1,0:T(4,128)} %param.4) | copy-start | bytes 12292
  0.6 0.9 %copy-start = (f32[2,2,4,128]{3,2,1,0:T(4,128)S(1)}, f32[2,2,4,128]{3,2,1,0:T(4,128)}, u32[]{:S(2)}) copy-start(f32[2,2,4,128]{3,2,1,0:T(4,128)} %param.3) | copy-start | bytes 24580
  2.0 1.4 %collective-permute-start = (f32[7,8,128]{2,1,0:T(8,128)S(1)}, f32[7,8,128]{2,1,0:T(8,128)S(1)}, u32[]{:S(2)}, u32[]{:S(2)}) collective-permute-start(f32[7,8,128]{2,1,0:T(8,128)S(1)} %get-tuple-element.11.own), channel_id=1, source_target_pairs={{0,4},{1,5},{2,6},{3,7},{4,0},{5,1},{6,2},{7,3},{8,12},{9,13},{10,... | collective-permute-start | bytes 86024 | tf_op jit(solution)/shard_map/ppermute | solution.py:390
  3.5 4.2 %collective-permute-start.1 = (f32[7,8,128]{2,1,0:T(8,128)S(1)}, f32[7,8,128]{2,1,0:T(8,128)S(1)}, u32[]{:S(2)}, u32[]{:S(2)}) collective-permute-start(f32[7,8,128]{2,1,0:T(8,128)S(1)} %maximum_maximum_fusion), channel_id=1, source_target_pairs={{0,12},{1,13},{2,14},{3,15},{4,8},{5,9},{6,10},{7,11},{8,4},{9,5},... | collective-permute-start | bytes 86024 | tf_op jit(solution)/shard_map/ppermute | solution.py:390
  7.7 3.4 %collective-permute-start.2 = (f32[7,8,128]{2,1,0:T(8,128)S(1)}, f32[7,8,128]{2,1,0:T(8,128)S(1)}, u32[]{:S(2)}, u32[]{:S(2)}) collective-permute-start(f32[7,8,128]{2,1,0:T(8,128)S(1)} %pad_maximum_fusion), channel_id=1, source_target_pairs={{0,20},{1,21},{2,22},{3,23},{4,16},{5,17},{6,18},{7,19},{8,28},{9,... | collective-permute-start | bytes 86024 | tf_op jit(solution)/shard_map/ppermute | solution.py:390
  11.2 3.5 %collective-permute-start.3 = (f32[10,8,128]{2,1,0:T(8,128)S(1)}, f32[10,8,128]{2,1,0:T(8,128)S(1)}, u32[]{:S(2)}, u32[]{:S(2)}) collective-permute-start(f32[10,8,128]{2,1,0:T(8,128)S(1)} %get-tuple-element.14), channel_id=1, source_target_pairs={{0,5},{1,4},{2,7},{3,6},{4,1},{5,0},{6,3},{7,2},{8,13},{9,12},{10,... | collective-permute-start | bytes 122888 | tf_op jit(solution)/shard_map/ppermute | solution.py:390
  14.8 7.8 %collective-permute-start.4 = (f32[7,8,128]{2,1,0:T(8,128)S(1)}, f32[7,8,128]{2,1,0:T(8,128)S(1)}, u32[]{:S(2)}, u32[]{:S(2)}) collective-permute-start(f32[7,8,128]{2,1,0:T(8,128)S(1)} %pad_maximum_fusion.2), channel_id=1, source_target_pairs={{0,6},{1,7},{2,4},{3,5},{4,2},{5,3},{6,0},{7,1},{8,14},{9,15},{10,... | collective-permute-start | bytes 86024 | tf_op jit(solution)/shard_map/ppermute | solution.py:390

commit v3 on v2

--- a/solution.py
+++ b/solution.py
@@ -146,7 +146,7 @@
     return total[0] - offset_y * weight, total[1] + offset_x * weight
 
 
-def near_sum(sources, targets, links, turned):
+def near_sum(sources, targets, links, turned, most=48):
     slots = sources[0][0].shape[1]
     stack = [part for source in sources for part in source]
     pad = -len(stack) % 8
@@ -156,7 +156,7 @@
 
     def step(k, totals):
         totals = list(totals)
-        chunk = turned[pl.ds(pl.multiple_of(8 * k, 8), 8), :]
+        chunk = turned[pl.ds(8 * k if isinstance(k, int) else pl.multiple_of(8 * k, 8), 8), :]
         for i, reached in enumerate(links):
             source = tuple(
                 jnp.broadcast_to(chunk[:, 3 * i + part : 3 * i + part + 1], (8, slots))
@@ -172,7 +172,7 @@
     pairs = sum(len(reached) for reached in links)
     chunks = slots // 8
     group = 1
-    while group * 2 * pairs <= 48 and chunks % (group * 2) == 0:
+    while group * 2 * pairs <= most and chunks % (group * 2) == 0:
         group *= 2
 
     def grouped(k, totals):
@@ -180,7 +180,11 @@
             totals = step(k * group + u, totals)
         return totals
 
-    totals = lax.fori_loop(0, chunks // group, grouped, (zero,) * (2 * len(targets)))
+    totals = (zero,) * (2 * len(targets))
+    if group == chunks:
+        totals = grouped(0, totals)
+    else:
+        totals = lax.fori_loop(0, chunks // group, grouped, totals)
     return [jnp.sum(total, axis=0, keepdims=True) for total in totals]
 
 
@@ -190,6 +194,42 @@
 
 def read_row(ref, base, at):
     return tuple(ref[base + part, pl.ds(at, 1), :] for part in range(3))
+
+
+def near_last_cols(rows, cols, side, spread, core, right, near):
+    slots = side.shape[2]
+    shift = jnp.where(right == 1, unit * cols, -unit * cols)
+    sources = []
+    for k in range(rows + 2):
+        row = read_row(side, 4, core * rows + k)
+        row = (row[0] + shift, row[1], row[2])
+        sources.append(tuple(jnp.broadcast_to(part, (8, slots)) for part in row))
+    stack = []
+    for r in range(rows):
+        parts = ([], [])
+        for k in range(slots // 8):
+            target = tuple(spread[2 * r + part, 8 * k : 8 * k + 8] for part in range(2))
+            total = (0.0, 0.0)
+            for i in range(r, r + 3):
+                total = pair_terms(target, sources[i], total)
+            parts[0].append(total[0])
+            parts[1].append(total[1])
+        stack += parts[0] + parts[1]
+    high, low = split(jnp.concatenate(stack, axis=0))
+    ones = jnp.ones((8, slots), jnp.bfloat16)
+
+    def lanes_sum(value):
+        return lax.dot_general(
+            ones, value, (((1,), (1,)), ((), ())), preferred_element_type=jnp.float32
+        )
+
+    sums = lanes_sum(high) + lanes_sum(low)
+    edge = jnp.where(right == 1, cols - 1, 0)
+    for r in range(rows):
+        for part in range(2):
+            at = pl.ds(r * cols + edge, 1)
+            lanes = slice((2 * r + part) * slots, (2 * r + part + 1) * slots)
+            near[part, at, :] = near[part, at, :] + sums[0:1, lanes]
 
 
 def near_local(rows, cols, own, cells, near, turned):
@@ -231,7 +271,7 @@
             near[part, at, :] = near[part, at, :] + sums[2 * c + part]
 
 
-def near_cols(rows, cols, own, side, base, core, right, near, turned):
+def near_cols(rows, cols, own, side, base, core, right, near, turned, most=48):
     shift = jnp.where(right == 1, unit * cols, -unit * cols)
     sources = []
     for k in range(rows + 2):
@@ -240,7 +280,7 @@
     edge = jnp.where(right == 1, cols - 1, 0)
     targets = [read_row(own, 4, r * cols + edge)[:2] for r in range(rows)]
     links = [[r for r in range(rows) if 0 <= k - r <= 2] for k in range(rows + 2)]
-    sums = near_sum(sources, targets, links, turned)
+    sums = near_sum(sources, targets, links, turned, most)
     for r in range(rows):
         for part in range(2):
             at = pl.ds(r * cols + edge, 1)
@@ -260,7 +300,7 @@
     near_rows(rows, cols, own, ring, 0, 1 - place[2], near, turned)
 
 
-def near_close_kernel(rows, cols, cell_count, own, close, near, weights, turned):
+def near_close_kernel(rows, cols, cell_count, own, close, near, weights, spread, turned):
     shape = (HALF, 2 * MODES)
     lane = lax.broadcasted_iota(jnp.int32, shape, 1)
     m = lax.broadcasted_iota(jnp.int32, shape, 0).astype(jnp.float32)
@@ -277,6 +317,12 @@
     place = position()
     near[...] = jnp.zeros_like(near)
     right = 1 - lax.rem(place[1], 2)
+    slots = own.shape[2]
+    edge = jnp.where(right == 1, 0, cols - 1)
+    for r in range(rows):
+        for part in range(2):
+            row = own[4 + part, pl.ds(r * cols + edge, 1), :]
+            spread[2 * r + part] = jnp.broadcast_to(row, (slots, slots)).T
     near_cols(rows, cols, own, close, 0, place[2], right, near, turned)
 
 
@@ -298,7 +344,7 @@
 
 def final_kernel(
     rows, cols, kept, own, x_table, y_table, last,
-    near_a, near_b, near_c, near_d, near_e, weights, velocity, moved, near, far, turned,
+    near_a, near_b, near_c, near_d, near_e, weights, spread, velocity, moved, near, far,
 ):
     cells = rows * cols
     slots = own.shape[2]
@@ -329,7 +375,7 @@
         far[0, pl.ds(i, 1), :] = jnp.sum(terms[0:MODES, lanes] * wave, axis=0, keepdims=True)
         far[1, pl.ds(i, 1), :] = jnp.sum(terms[MODES:, lanes] * wave, axis=0, keepdims=True)
     near[...] = (near_a[...] + near_b[...]) + (near_c[...] + near_d[...]) + near_e[...]
-    near_cols(rows, cols, own, last, 4, core, lax.rem(place[1], 2), near, turned)
+    near_last_cols(rows, cols, last, spread, core, lax.rem(place[1], 2), near)
     live = kept[3] > 0.5
     for part in range(2):
         value = jnp.where(live, near[part] + far[part], 0.0)
@@ -405,10 +451,13 @@
     bit = 1
     while bit < chips:
         message = jnp.concatenate([total, items[-1]], axis=0)
-        got = swap(message, bit, 0)
-        total = total + got[0:4]
-        items.append(got[4:7])
-        bit *= 2
+        steps = (1, 2, 3) if 4 * bit <= chips else (1,)
+        for step in steps:
+            got = swap(message, step * bit, 0)
+            total = total + got[0:4]
+            if step != 2:
+                items.append(got[4:7])
+        bit *= len(steps) + 1
     near_b = near_call(
         functools.partial(near_local_kernel, rows, cols, whole[third : 3 * third]), 9_000_000, own
     )
@@ -440,9 +489,10 @@
         total = total + got[0:4]
         items.append(got[4:7])
         bit *= 2
-    near_e, weights = call(
+    near_e, weights, spread = call(
         functools.partial(near_close_kernel, rows, cols, cell_count),
-        near_shape + [((2, HALF, 2 * MODES), f32)], turned, 3_000_000,
+        near_shape + [((2, HALF, 2 * MODES), f32), ((2 * rows, slots, slots), f32)],
+        turned, 3_000_000,
         own, close,
     )
     distant = far_item(items, ty) if ty_size > 2 else items[1]
@@ -451,10 +501,10 @@
         call(
             functools.partial(final_kernel, rows, cols),
             [(offsets.shape, f32)] * 2,
-            [pltpu.VMEM((2, cells, slots), f32), pltpu.VMEM((2, cells, slots), f32)] + turned,
+            [pltpu.VMEM((2, cells, slots), f32), pltpu.VMEM((2, cells, slots), f32)],
             4_000_000,
             kept, own, x_table, y_table, last,
-            near_a, near_b, near_c, near_d, near_e, weights,
+            near_a, near_b, near_c, near_d, near_e, weights, spread,
         )
     )
 

time: 24.2 us -> 23.3 us (0.963)
  starting transfers between devices: 9.82 us -> 8.6 us
  waiting for transfers between devices: 5.64 us -> 6.15 us
  Pallas kernels: 6.76 us -> 6.5 us
    ppermute x5 -> x6, starting transfers between devices: 9.82 us -> 8.6 us  [swap(): return lax.ppermute(message, ('tx', 'ty'), pairs)]
    ppermute x5 -> x6, waiting for transfers between devices: 5.64 us -> 6.15 us  [swap(): return lax.ppermute(message, ('tx', 'ty'), pairs)]
    pallas_call x8, Pallas kernels: 6.76 us -> 6.5 us  [call(): pl.pallas_call(body, out_shape=outs, in_specs=[VMEM] * len(args), out_spe...]
  transfers between devices with their start and end apart: 5 -> 6, of which waited for: 4 -> 5; matrix products, arithmetic and copies ran while one was open for 0% -> 0% of each run, Pallas kernels for 20% -> 21%
where the time goes in v3:
time: 23.3 us; the launch traced here: 23.1 us
  starting transfers between devices  8.6 us (37%)
  Pallas kernels  6.5 us (28%)
  waiting for transfers between devices  6.15 us (26%)
  other arithmetic  1.02 us (4%)
  between operations  0.81 us (3%)
    ppermute x6, starting transfers between devices, swap(): return lax.ppermute(message, ('tx', 'ty'), pairs)  8.6 us
    pallas_call x8, Pallas kernels, call(): pl.pallas_call(body, out_shape=outs, in_specs=[VMEM] * len(args), out_spe...  6.5 us
    ppermute x6, waiting for transfers between devices, swap(): return lax.ppermute(message, ('tx', 'ty'), pairs)  6.15 us
    select_n x1, other arithmetic, per_device(): jnp.where(live, 1.0, 0.0)  0.79 us
  transfers between devices with their start and end apart: 6, of which 5 were waited for; matrix products, arithmetic and copies ran while one was open for 0% of the time, Pallas kernels for 21%

profile of v3, /device:TPU:0, one launch (start us, length us, event | category | flops | bytes accessed | tf_op | source)
XLA Modules:
  0.0 23.1 jit_solution(9870934992870841636)
XLA Ops:
  0.6 0.0 copy-start.1
  0.7 0.8 %fusion.1 = f32[1,2,4,128]{3,2,1,0:T(4,128)S(1)} fusion(s32[2,4]{1,0:T(2,128)} %param.5), kind=kLoop, calls=%fused_computation.20 | loop fusion | flops 2048 | bytes 4128 | tf_op jit(solution)/shard_map/jit(_where)/select_n | solution.py:412
  1.5 0.0 copy-done.2
  1.5 0.1 select_bitcast_fusion
  1.5 0.5 %shard_map.50 = (f32[7,8,128]{2,1,0:T(8,128)S(1)}, f32[4,8,128]{2,1,0:T(8,128)S(1)}, f32[64,1024]{1,0:T(8,128)S(1)}, bf16[128,1024]{1,0:T(8,128)(2,1)S(1)}) custom-call(f32[4,2,4,128]{3,2,1,0:T(4,128)S(1)} %pad_maximum_fusion.3.slot_state), custom_call_target="tpu_custom_call" | custom-call | flops 4000000 | bytes 65536 | tf_op jit(solution)/shard_map/pallas_call | solution.py:33
  2.0 0.6 %collective-permute-start = (f32[7,8,128]{2,1,0:T(8,128)S(1)}, f32[7,8,128]{2,1,0:T(8,128)S(1)}, u32[]{:S(2)}, u32[]{:S(2)}) collective-permute-start(f32[7,8,128]{2,1,0:T(8,128)S(1)} %get-tuple-element.12.own), channel_id=1, source_target_pairs={{0,4},{1,5},{2,6},{3,7},{4,0},{5,1},{6,2},{7,3},{8,12},{9,13},{10,... | collective-permute-start | bytes 86024 | tf_op jit(solution)/shard_map/ppermute | solution.py:436
  2.6 0.8 %collective-permute-done.partner = f32[7,8,128]{2,1,0:T(8,128)S(1)} collective-permute-done((f32[7,8,128]{2,1,0:T(8,128)S(1)}, f32[7,8,128]{2,1,0:T(8,128)S(1)}, u32[]{:S(2)}, u32[]{:S(2)}) %collective-permute-start) | collective-permute-done | bytes 28704 | tf_op jit(solution)/shard_map/ppermute | solution.py:436
  3.5 3.6 %collective-permute-start.3 = (f32[7,8,128]{2,1,0:T(8,128)S(1)}, f32[7,8,128]{2,1,0:T(8,128)S(1)}, u32[]{:S(2)}, u32[]{:S(2)}) collective-permute-start(f32[7,8,128]{2,1,0:T(8,128)S(1)} %maximum_maximum_fusion), channel_id=1, source_target_pairs={{0,28},{1,29},{2,30},{3,31},{4,24},{5,25},{6,26},{7,27},{8,20},{9,... | collective-permute-start | bytes 86024 | tf_op jit(solution)/shard_map/ppermute | solution.py:436
  7.1 0.5 %collective-permute-start.2 = (f32[7,8,128]{2,1,0:T(8,128)S(1)}, f32[7,8,128]{2,1,0:T(8,128)S(1)}, u32[]{:S(2)}, u32[]{:S(2)}) collective-permute-start(f32[7,8,128]{2,1,0:T(8,128)S(1)} %maximum_maximum_fusion), channel_id=1, source_target_pairs={{0,20},{1,21},{2,22},{3,23},{4,16},{5,17},{6,18},{7,19},{8,28},{9,... | collective-permute-start | bytes 86024 | tf_op jit(solution)/shard_map/ppermute | solution.py:436
  7.6 0.1 collective-permute-start.1
  7.7 1.0 %collective-permute-done.3 = f32[7,8,128]{2,1,0:T(8,128)S(1)} collective-permute-done((f32[7,8,128]{2,1,0:T(8,128)S(1)}, f32[7,8,128]{2,1,0:T(8,128)S(1)}, u32[]{:S(2)}, u32[]{:S(2)}) %collective-permute-start.3) | collective-permute-done | bytes 28704 | tf_op jit(solution)/shard_map/ppermute | solution.py:436
  8.7 1.7 %collective-permute-done.2 = f32[7,8,128]{2,1,0:T(8,128)S(1)} collective-permute-done((f32[7,8,128]{2,1,0:T(8,128)S(1)}, f32[7,8,128]{2,1,0:T(8,128)S(1)}, u32[]{:S(2)}, u32[]{:S(2)}) %collective-permute-start.2) | collective-permute-done | bytes 28704 | tf_op jit(solution)/shard_map/ppermute | solution.py:436
  10.4 0.5 %collective-permute-done.1 = f32[7,8,128]{2,1,0:T(8,128)S(1)} collective-permute-done((f32[7,8,128]{2,1,0:T(8,128)S(1)}, f32[7,8,128]{2,1,0:T(8,128)S(1)}, u32[]{:S(2)}, u32[]{:S(2)}) %collective-permute-start.1) | collective-permute-done | bytes 28704 | tf_op jit(solution)/shard_map/ppermute | solution.py:436
  10.9 0.1 fusion
  11.0 1.4 %collective-permute-start.4 = (f32[10,8,128]{2,1,0:T(8,128)S(1)}, f32[10,8,128]{2,1,0:T(8,128)S(1)}, u32[]{:S(2)}, u32[]{:S(2)}) collective-permute-start(f32[10,8,128]{2,1,0:T(8,128)S(1)} %get-tuple-element.15), channel_id=1, source_target_pairs={{0,5},{1,4},{2,7},{3,6},{4,1},{5,0},{6,3},{7,2},{8,13},{9,12},{10,... | collective-permute-start | bytes 122888 | tf_op jit(solution)/shard_map/ppermute | solution.py:436
  12.4 2.2 %collective-permute-done.4 = f32[10,8,128]{2,1,0:T(8,128)S(1)} collective-permute-done((f32[10,8,128]{2,1,0:T(8,128)S(1)}, f32[10,8,128]{2,1,0:T(8,128)S(1)}, u32[]{:S(2)}, u32[]{:S(2)}) %collective-permute-start.4) | collective-permute-done | bytes 40992 | tf_op jit(solution)/shard_map/ppermute | solution.py:436
  14.6 2.4 %collective-permute-start.5 = (f32[7,8,128]{2,1,0:T(8,128)S(1)}, f32[7,8,128]{2,1,0:T(8,128)S(1)}, u32[]{:S(2)}, u32[]{:S(2)}) collective-permute-start(f32[7,8,128]{2,1,0:T(8,128)S(1)} %pad_maximum_fusion.1), channel_id=1, source_target_pairs={{0,6},{1,7},{2,4},{3,5},{4,2},{5,3},{6,0},{7,1},{8,14},{9,15},{10,... | collective-permute-start | bytes 86024 | tf_op jit(solution)/shard_map/ppermute | solution.py:436
  17.0 0.6 %shard_map.52.near_a = f32[2,8,128]{2,1,0:T(8,128)S(1)} custom-call(f32[7,8,128]{2,1,0:T(8,128)S(1)} %get-tuple-element.12.own), custom_call_target="tpu_custom_call" | custom-call | flops 4000000 | bytes 65536 | tf_op jit(solution)/shard_map/pallas_call | solution.py:33
  17.7 1.4 %shard_map.53.near_b = f32[2,8,128]{2,1,0:T(8,128)S(1)} custom-call(f32[7,8,128]{2,1,0:T(8,128)S(1)} %get-tuple-element.12.own), custom_call_target="tpu_custom_call" | custom-call | flops 9000000 | bytes 65536 | tf_op jit(solution)/shard_map/pallas_call | solution.py:33
  19.1 1.4 %shard_map.54.near_c = f32[2,8,128]{2,1,0:T(8,128)S(1)} custom-call(f32[7,8,128]{2,1,0:T(8,128)S(1)} %get-tuple-element.12.own, f32[7,8,128]{2,1,0:T(8,128)S(1)} %collective-permute-done.partner), custom_call_target="tpu_custom_call" | custom-call | flops 9000000 | bytes 65536 | tf_op jit(solution)/shard_map/pallas_call | solution.py:33
  20.5 0.8 %shard_map.55.near_d = f32[2,8,128]{2,1,0:T(8,128)S(1)} custom-call(f32[7,8,128]{2,1,0:T(8,128)S(1)} %get-tuple-element.12.own, f32[3,8,128]{2,1,0:T(8,128)S(1)} %get-tuple-element.16.ring), custom_call_target="tpu_custom_call" | custom-call | flops 5000000 | bytes 65536 | tf_op jit(solution)/shard_map/pallas_call | solution.py:33
  21.3 0.7 %shard_map.56 = (f32[2,8,128]{2,1,0:T(8,128)S(1)}, f32[2,32,128]{2,1,0:T(8,128)S(1)}, f32[4,128,128]{2,1,0:T(8,128)S(1)}) custom-call(f32[7,8,128]{2,1,0:T(8,128)S(1)} %get-tuple-element.12.own, f32[3,8,128]{2,1,0:T(8,128)S(1)} %get-tuple-element.20.close), custom_call_target="tpu_custom_call" | custom-call | flops 3000000 | bytes 65536 | tf_op jit(solution)/shard_map/pallas_call | solution.py:33
  21.9 0.0 collective-permute-done.5
  22.0 1.1 %shard_map.57 = (f32[2,2,4,128]{3,2,1,0:T(4,128)}, f32[2,2,4,128]{3,2,1,0:T(4,128)}) custom-call(f32[4,8,128]{2,1,0:T(8,128)S(1)} %get-tuple-element.11.kept, f32[7,8,128]{2,1,0:T(8,128)S(1)} %get-tuple-element.12.own, f32[64,1024]{1,0:T(8,128)S(1)} %get-tuple-element.13.x_table, bf16[128,1024]{1,0:T(8,128)(2,1)S(1)} %get-tuple-element.14.y_table, ...), custom_call_target="tpu_custom_call" | custom-call | flops 4000000 | bytes 65536 | tf_op jit(solution)/shard_map/pallas_call | solution.py:33
  (22 shorter events, 0.1 us)
Async XLA Ops:
  0.6 0.8 %copy-start.1 = (s32[2,4]{1,0:T(2,128)S(1)}, s32[2,4]{1,0:T(2,128)}, u32[]{:S(2)}) copy-start(s32[2,4]{1,0:T(2,128)} %param.5) | copy-start | bytes 100
  0.6 0.8 %copy-start.2 = (f32[2,4,128]{2,1,0:T(4,128)S(1)}, f32[2,4,128]{2,1,0:T(4,128)}, u32[]{:S(2)}) copy-start(f32[2,4,128]{2,1,0:T(4,128)} %param.4) | copy-start | bytes 12292
  0.6 0.9 %copy-start = (f32[2,2,4,128]{3,2,1,0:T(4,128)S(1)}, f32[2,2,4,128]{3,2,1,0:T(4,128)}, u32[]{:S(2)}) copy-start(f32[2,2,4,128]{3,2,1,0:T(4,128)} %param.3) | copy-start | bytes 24580
  2.0 1.4 %collective-permute-start = (f32[7,8,128]{2,1,0:T(8,128)S(1)}, f32[7,8,128]{2,1,0:T(8,128)S(1)}, u32[]{:S(2)}, u32[]{:S(2)}) collective-permute-start(f32[7,8,128]{2,1,0:T(8,128)S(1)} %get-tuple-element.12.own), channel_id=1, source_target_pairs={{0,4},{1,5},{2,6},{3,7},{4,0},{5,1},{6,2},{7,3},{8,12},{9,13},{10,... | collective-permute-start | bytes 86024 | tf_op jit(solution)/shard_map/ppermute | solution.py:436
  3.5 5.2 %collective-permute-start.3 = (f32[7,8,128]{2,1,0:T(8,128)S(1)}, f32[7,8,128]{2,1,0:T(8,128)S(1)}, u32[]{:S(2)}, u32[]{:S(2)}) collective-permute-start(f32[7,8,128]{2,1,0:T(8,128)S(1)} %maximum_maximum_fusion), channel_id=1, source_target_pairs={{0,28},{1,29},{2,30},{3,31},{4,24},{5,25},{6,26},{7,27},{8,20},{9,... | collective-permute-start | bytes 86024 | tf_op jit(solution)/shard_map/ppermute | solution.py:436
  7.1 3.3 %collective-permute-start.2 = (f32[7,8,128]{2,1,0:T(8,128)S(1)}, f32[7,8,128]{2,1,0:T(8,128)S(1)}, u32[]{:S(2)}, u32[]{:S(2)}) collective-permute-start(f32[7,8,128]{2,1,0:T(8,128)S(1)} %maximum_maximum_fusion), channel_id=1, source_target_pairs={{0,20},{1,21},{2,22},{3,23},{4,16},{5,17},{6,18},{7,19},{8,28},{9,... | collective-permute-start | bytes 86024 | tf_op jit(solution)/shard_map/ppermute | solution.py:436
  7.6 3.3 %collective-permute-start.1 = (f32[7,8,128]{2,1,0:T(8,128)S(1)}, f32[7,8,128]{2,1,0:T(8,128)S(1)}, u32[]{:S(2)}, u32[]{:S(2)}) collective-permute-start(f32[7,8,128]{2,1,0:T(8,128)S(1)} %maximum_maximum_fusion), channel_id=1, source_target_pairs={{0,12},{1,13},{2,14},{3,15},{4,8},{5,9},{6,10},{7,11},{8,4},{9,5},... | collective-permute-start | bytes 86024 | tf_op jit(solution)/shard_map/ppermute | solution.py:436
  11.0 3.6 %collective-permute-start.4 = (f32[10,8,128]{2,1,0:T(8,128)S(1)}, f32[10,8,128]{2,1,0:T(8,128)S(1)}, u32[]{:S(2)}, u32[]{:S(2)}) collective-permute-start(f32[10,8,128]{2,1,0:T(8,128)S(1)} %get-tuple-element.15), channel_id=1, source_target_pairs={{0,5},{1,4},{2,7},{3,6},{4,1},{5,0},{6,3},{7,2},{8,13},{9,12},{10,... | collective-permute-start | bytes 122888 | tf_op jit(solution)/shard_map/ppermute | solution.py:436
  14.6 7.3 %collective-permute-start.5 = (f32[7,8,128]{2,1,0:T(8,128)S(1)}, f32[7,8,128]{2,1,0:T(8,128)S(1)}, u32[]{:S(2)}, u32[]{:S(2)}) collective-permute-start(f32[7,8,128]{2,1,0:T(8,128)S(1)} %pad_maximum_fusion.1), channel_id=1, source_target_pairs={{0,6},{1,7},{2,4},{3,5},{4,2},{5,3},{6,0},{7,1},{8,14},{9,15},{10,... | collective-permute-start | bytes 86024 | tf_op jit(solution)/shard_map/ppermute | solution.py:436
